TPU v7x, 512 devices: a whole 4x4x16 slice. The times are simulated.
512 devices in a mesh: ta: 8 (over z_hi, x), ha: 64 (over y, z_lo, core).
Axes of the slice: x: 4, y: 4, z: 16 (z_hi: 2, z_lo: 8; z = z_hi * 8 + z_lo), core: 2. Of those that a mesh axis runs over, the one named last changes fastest.
Arguments:
- query: bfloat16 [64, 64, 16, 2560], P('ta', 'ha'), may hold values from -2.5 to 2.5
- key_value: bfloat16 [64, 64, 16, 5120], P('ta', 'ha'), may hold values from -2.5 to 2.5
- out_grad: bfloat16 [64, 64, 16, 2560], P('ta', 'ha'), may hold values from -96 to 96
- text_kv: bfloat16 [32, 5120], replicated, may hold values from -2.5 to 2.5
- tile_reach: int32 [64, 64, 2], replicated, may hold values from 0 to 1
- text_len: int32 [64, 64], replicated, may hold values from 1 to 32
Outputs:
- query_grad: bfloat16 [64, 64, 16, 2560], P('ta', 'ha')
- key_value_grad: bfloat16 [64, 64, 16, 5120], P('ta', 'ha')
- text_grad: bfloat16 [32, 5120], P(None, ('ta', 'ha'))
Inputs may be any that keep to these rules, and one draw needn't show every extreme that they name: tile_reach[f, r, 0] and tile_reach[f, r, 1] are the frames and rows that the window of the tile at (f, r) reaches to each side. The tile at (f, r) sees the first text_len[f, r] text tokens.
All inputs are finite; a program needn't handle non-finite values.
Results may differ from a plain program's by a relative error of at most 0.008.
Values may be sent and summed in bfloat16 or wider, within the bound.
A program may use at most 128 MiB of HBM per device.

v0:
```python
import math

import jax
import jax.numpy as jnp
from jax import lax
from jax.sharding import PartitionSpec as P

HD = 128


def passed_along(block, axis, distance):
    devices = range(lax.axis_size(axis))
    route = [(i - distance, i) for i in devices if i - distance in devices]
    return lax.ppermute(block, axis, route)


def for_sending(x):
    return jax.tree.map(lambda a: a.astype(jnp.bfloat16) if a.dtype == jnp.float32 else a, x)


def padded(block, sides, width):
    for axis, dim in sides:
        count = lax.axis_size(axis)
        forward = [(i, i + 1) for i in range(count - 1)]
        backward = [(target, source) for source, target in forward]
        low = lax.ppermute(
            lax.slice_in_dim(block, block.shape[dim] - width, None, axis=dim), axis, forward
        )
        high = lax.ppermute(lax.slice_in_dim(block, 0, width, axis=dim), axis, backward)
        block = jnp.concatenate([low, block, high], axis=dim)
    return block


def fold_rows(grad_ext):
    middle = grad_ext[:, 1]
    for offset, slab_index in ((1, 2), (-1, 0)):
        middle = middle + passed_along(
            grad_ext[:, slab_index].astype(jnp.bfloat16), "ha", offset
        ).astype(jnp.float32)
    return middle[:, None]


def fold_frames(grad_ext):
    interior = grad_ext[1:-1]
    for offset, source, target in ((1, -1, 0), (-1, 0, -1)):
        arrived = passed_along(for_sending(grad_ext[source]), "ta", offset)
        interior = interior.at[target].add(arrived)
    return interior


def on_device(query, key_value, out_grad, text_kv, tile_reach, text_len):
    frames_dev = query.shape[0]
    columns = query.shape[2]
    feature_width = query.shape[3]
    head_count = feature_width // HD
    text_count = text_kv.shape[0]
    tokens = frames_dev * columns
    band = 3 * columns
    score_scale = 1.0 / math.sqrt(HD)
    time_index = lax.axis_index("ta")
    row_index = lax.axis_index("ha")
    frame_total = frames_dev * lax.axis_size("ta")
    row_total = lax.axis_size("ha")
    first_frame = time_index * frames_dev
    own_reach = lax.dynamic_slice(tile_reach, (first_frame, row_index, 0), (frames_dev, 1, 2))[:, 0]
    own_length = lax.dynamic_slice(text_len, (first_frame, row_index), (frames_dev, 1))[:, 0]
    ext_count = frames_dev + 2
    ext_frame = jnp.arange(ext_count, dtype=jnp.int32) - 1
    ext_row = jnp.arange(3, dtype=jnp.int32) - 1
    step_shift = jnp.arange(3, dtype=jnp.int32) - 1
    own_frame = jnp.arange(frames_dev, dtype=jnp.int32)
    frame_inside = (first_frame + ext_frame >= 0) & (first_frame + ext_frame < frame_total)
    row_inside = (row_index + ext_row >= 0) & (row_index + ext_row < row_total)
    near_index = own_frame[:, None] + jnp.arange(3, dtype=jnp.int32)[None, :]
    frame_ok = frame_inside[near_index] & (jnp.abs(step_shift)[None, :] <= own_reach[:, 0:1])
    row_ok = row_inside[None, :] & (jnp.abs(ext_row)[None, :] <= own_reach[:, 1:2])
    tile_ok = frame_ok[:, :, None] & row_ok[:, None, :]
    window_mask = jnp.broadcast_to(tile_ok[:, :, :, None], (frames_dev, 3, 3, columns)).reshape(
        frames_dev, 9 * columns
    )[:, None, None, :]
    text_open = jnp.arange(text_count, dtype=jnp.int32)[:, None, None] < own_length[None, :, None]
    text_mask = jnp.broadcast_to(text_open, (text_count, frames_dev, columns)).reshape(
        text_count, tokens
    )
    query_heads = query.reshape(tokens, head_count, HD)
    grad_heads = out_grad.reshape(tokens, head_count, HD)
    query_four = query.reshape(frames_dev, columns, head_count, HD)
    grad_four = out_grad.reshape(frames_dev, columns, head_count, HD)
    extended = padded(key_value, (("ta", 0), ("ha", 1)), 1)
    keys_ext = extended[..., :feature_width].reshape(ext_count, band, head_count, HD)
    values_ext = extended[..., feature_width:].reshape(ext_count, band, head_count, HD)
    text_keys = text_kv[:, :feature_width].reshape(text_count, head_count, HD)
    text_values = text_kv[:, feature_width:].reshape(text_count, head_count, HD)
    win_scores = (
        jnp.concatenate(
            [
                jnp.einsum(
                    "fqhd,fkhd->fhqk",
                    query_four,
                    keys_ext[step : step + frames_dev],
                    preferred_element_type=jnp.float32,
                )
                for step in range(3)
            ],
            axis=-1,
        )
        * score_scale
    )
    txt_scores = (
        jnp.einsum("qhd,khd->hkq", query_heads, text_keys, preferred_element_type=jnp.float32)
        * score_scale
    )
    win_total = jnp.sum(jnp.where(window_mask, jnp.exp(win_scores), 0.0), axis=-1)
    win_total = jnp.transpose(win_total, (1, 0, 2)).reshape(head_count, tokens)
    exp_total = win_total + jnp.sum(jnp.where(text_mask[None], jnp.exp(txt_scores), 0.0), axis=1)
    log_total = jnp.log(exp_total)
    log_four = jnp.transpose(log_total.reshape(head_count, frames_dev, columns), (1, 0, 2))
    win_prob = jnp.where(window_mask, jnp.exp(win_scores - log_four[..., None]), 0.0)
    txt_prob = jnp.where(text_mask[None], jnp.exp(txt_scores - log_total[:, None, :]), 0.0)
    win_half = win_prob.astype(jnp.bfloat16)
    txt_half = txt_prob.astype(jnp.bfloat16)
    attended = win_half[..., 0:band] * 0.0
    attended = sum(
        (
            jnp.einsum(
                "fhqk,fkhd->fqhd",
                win_half[..., step * band : (step + 1) * band],
                values_ext[step : step + frames_dev],
                preferred_element_type=jnp.float32,
            )
            for step in range(3)
        )
    )
    attended = attended.reshape(tokens, head_count, HD) + jnp.einsum(
        "hkq,khd->qhd", txt_half, text_values, preferred_element_type=jnp.float32
    )
    row_delta = jnp.sum(grad_heads.astype(jnp.float32) * attended, axis=-1).T
    delta_four = jnp.transpose(row_delta.reshape(head_count, frames_dev, columns), (1, 0, 2))
    win_dprob = jnp.concatenate(
        [
            jnp.einsum(
                "fqhd,fkhd->fhqk",
                grad_four,
                values_ext[step : step + frames_dev],
                preferred_element_type=jnp.float32,
            )
            for step in range(3)
        ],
        axis=-1,
    )
    win_dscore = (win_prob * (win_dprob - delta_four[..., None])).astype(jnp.bfloat16)
    query_sum = sum(
        (
            jnp.einsum(
                "fhqk,fkhd->fqhd",
                win_dscore[..., step * band : (step + 1) * band],
                keys_ext[step : step + frames_dev],
                preferred_element_type=jnp.float32,
            )
            for step in range(3)
        )
    )
    query_sum = query_sum.reshape(tokens, head_count, HD)
    contributions = []
    for step in range(3):
        key_part = (
            jnp.einsum(
                "fhqk,fqhd->fkhd",
                win_dscore[..., step * band : (step + 1) * band],
                query_four,
                preferred_element_type=jnp.float32,
            )
            * score_scale
        )
        value_part = jnp.einsum(
            "fhqk,fqhd->fkhd",
            win_half[..., step * band : (step + 1) * band],
            grad_four,
            preferred_element_type=jnp.float32,
        )
        joined = jnp.concatenate(
            [
                key_part.reshape(frames_dev, band, feature_width),
                value_part.reshape(frames_dev, band, feature_width),
            ],
            axis=-1,
        )
        contributions.append(jnp.pad(joined, ((step, 2 - step), (0, 0), (0, 0))))
    grad_ext = (contributions[0] + contributions[1] + contributions[2]).reshape(
        ext_count, 3, columns, 2 * feature_width
    )
    folded = fold_frames(fold_rows(grad_ext))
    key_value_grad = folded.astype(jnp.bfloat16)
    txt_dprob = jnp.einsum(
        "qhd,khd->hkq", grad_heads, text_values, preferred_element_type=jnp.float32
    )
    txt_dscore = (txt_prob * (txt_dprob - row_delta[:, None, :])).astype(jnp.bfloat16)
    query_sum = query_sum + jnp.einsum(
        "hkq,khd->qhd", txt_dscore, text_keys, preferred_element_type=jnp.float32
    )
    text_key_part = (
        jnp.einsum("hkq,qhd->khd", txt_dscore, query_heads, preferred_element_type=jnp.float32)
        * score_scale
    )
    text_value_part = jnp.einsum(
        "hkq,qhd->khd", txt_half, grad_heads, preferred_element_type=jnp.float32
    )
    text_partial = jnp.concatenate(
        [
            text_key_part.reshape(text_count, feature_width),
            text_value_part.reshape(text_count, feature_width),
        ],
        axis=1,
    )
    query_grad = (query_sum * score_scale).astype(jnp.bfloat16).reshape(query.shape)
    text_grad = lax.psum_scatter(
        text_partial, ("ta", "ha"), scatter_dimension=1, tiled=True
    ).astype(jnp.bfloat16)
    return (query_grad, key_value_grad, text_grad)


def solution(mesh):
    placed = (
        P("ta", "ha", None, None),
        P("ta", "ha", None, None),
        P("ta", "ha", None, None),
        P(),
        P(),
        P(),
    )
    return jax.shard_map(
        on_device,
        mesh=mesh,
        in_specs=placed,
        out_specs=(P("ta", "ha", None, None), P("ta", "ha", None, None), P(None, ("ta", "ha"))),
        check_vma=False,
    )
```

profile of v0, /device:TPU:289, one launch (start us, length us, event | category | flops | bytes accessed | tf_op | source)
XLA Modules:
  0.0 378.6 jit_solution(3081030261429648667)
XLA Ops:
  0.7 1.1 fusion.126
  1.7 1.9 collective-permute-start.1
  3.7 3.4 collective-permute-start
  7.2 14.2 %collective-permute-done = bf16[1,1,16,5120]{3,2,1,0:T(8,128)(2,1)S(1)} collective-permute-done((bf16[1,1,16,5120]{3,2,1,0:T(8,128)(2,1)S(1)}, bf16[1,1,16,5120]{3,2,1,0:T(8,128)(2,1)S(1)}, u32[]{:S(2)}, u32[]{:S(2)}) %collective-permute-start) | collective-permute-done | bytes 163872 | tf_op jit(solution)/shard_map/ppermute | solution.py:26
  22.1 2.5 constant_dynamic-update-slice_fusion.1
  25.3 14.2 %collective-permute-start.3 = (bf16[10,1,16,5120]{3,2,1,0:T(8,128)(2,1)}, bf16[10,1,16,5120]{3,2,1,0:T(8,128)(2,1)}, u32[]{:S(2)}, u32[]{:S(2)}) collective-permute-start(bf16[10,1,16,5120]{3,2,1,0:T(8,128)(2,1)} %constant_dynamic-update-slice_fusion), channel_id=1, source_target_pairs={{1,0},{2,1},{3,2},{4,3},{5,4},{6,5},{7,6},{8,7},{9,8},{10,9},{11,1... | collective-permute-start | bytes 4915208 | tf_op jit(solution)/shard_map/ppermute | solution.py:29
  39.5 1.9 collective-permute-start.2
  41.9 1.3 reshape.327
  44.0 0.9 dynamic-slice_reduce_fusion
  46.3 1.0 slice_bitcast_fusion.4
  47.4 1.7 select_reduce_fusion.1
  49.8 1.3 copy.100
  51.1 6.4 %collective-permute-done.3 = bf16[10,1,16,5120]{3,2,1,0:T(8,128)(2,1)} collective-permute-done((bf16[10,1,16,5120]{3,2,1,0:T(8,128)(2,1)}, bf16[10,1,16,5120]{3,2,1,0:T(8,128)(2,1)}, u32[]{:S(2)}, u32[]{:S(2)}) %collective-permute-start.3) | collective-permute-done | bytes 1638432 | tf_op jit(solution)/shard_map/ppermute | solution.py:29
  57.4 2.4 collective-permute-done.2
  59.8 2.9 pad_maximum_fusion
  62.8 4.6 %fusion.124 = (bf16[8,3,16,2560]{3,2,1,0:T(8,128)(2,1)}, bf16[8,3,16,2560]{3,2,1,0:T(8,128)(2,1)}, bf16[8,3,16,2560]{3,2,1,0:T(8,128)(2,1)}, bf16[8,3,16,2560]{3...) fusion(bf16[10,3,16,5120]{3,2,1,0:T(8,128)(2,1)S(1)} %pad_maximum_fusion), kind=kLoop, calls=%fused_computation.160 | loop fusion | bytes 23592960 | tf_op jit(solution)/shard_map/slice | solution.py:157
  67.3 4.3 %slice.179 = bf16[8,48,20,128]{3,2,1,0:T(8,128)(2,1)} reshape(bf16[8,3,16,2560]{3,2,1,0:T(8,128)(2,1)} %get-tuple-element.37) | data formatting | bytes 3932160 | tf_op jit(solution)/shard_map/slice | solution.py:157
  71.7 4.3 %slice.193 = bf16[8,48,20,128]{3,2,1,0:T(8,128)(2,1)} reshape(bf16[8,3,16,2560]{3,2,1,0:T(8,128)(2,1)} %get-tuple-element.38) | data formatting | bytes 3932160 | tf_op jit(solution)/shard_map/slice | solution.py:144
  76.0 4.4 %slice.191 = bf16[8,48,20,128]{3,2,1,0:T(8,128)(2,1)} reshape(bf16[8,3,16,2560]{3,2,1,0:T(8,128)(2,1)} %get-tuple-element.39) | data formatting | bytes 3932160 | tf_op jit(solution)/shard_map/slice | solution.py:144
  80.4 4.0 %fusion.66 = f32[8,20,16,48]{3,2,1,0:T(8,128)} fusion(bf16[8,48,20,128]{3,2,1,0:T(8,128)(2,1)} %slice.193, bf16[8,16,20,128]{3,2,1,0:T(8,128)(2,1)S(1)} %reshape.328), kind=kOutput, calls=%fused_computation.77 | convolution fusion | flops 31457280 | bytes 3112960 | tf_op jit(solution)/shard_map/fqhd,fkhd->fhqk/dot_general | solution.py:141
  84.4 2.2 fusion.63
  86.6 4.3 %slice.186 = bf16[8,48,20,128]{3,2,1,0:T(8,128)(2,1)} reshape(bf16[8,3,16,2560]{3,2,1,0:T(8,128)(2,1)} %get-tuple-element.41) | data formatting | bytes 3932160 | tf_op jit(solution)/shard_map/slice | solution.py:100
  90.9 2.9 fusion.69
  93.9 2.2 fusion.57
  96.1 4.4 %slice.184 = bf16[8,48,20,128]{3,2,1,0:T(8,128)(2,1)} reshape(bf16[8,3,16,2560]{3,2,1,0:T(8,128)(2,1)} %get-tuple-element.42) | data formatting | bytes 3932160 | tf_op jit(solution)/shard_map/slice | solution.py:100
  100.5 2.9 fusion.54
  103.4 1.8 select_reduce_fusion
  105.8 2.0 fusion.7
  107.9 1.8 fusion.12
  109.7 0.8 copy-done.14
  110.5 1.8 fusion.16
  112.3 4.4 %slice.189 = bf16[8,48,20,128]{3,2,1,0:T(8,128)(2,1)} reshape(bf16[8,3,16,2560]{3,2,1,0:T(8,128)(2,1)} %get-tuple-element.40) | data formatting | bytes 3932160 | tf_op jit(solution)/shard_map/slice | solution.py:144
  116.7 4.0 %fusion.60 = f32[8,20,16,48]{3,2,1,0:T(8,128)} fusion(bf16[8,48,20,128]{3,2,1,0:T(8,128)(2,1)} %slice.189, bf16[8,16,20,128]{3,2,1,0:T(8,128)(2,1)S(1)} %reshape.328), kind=kOutput, calls=%fused_computation.75 | convolution fusion | flops 31457280 | bytes 3112960 | tf_op jit(solution)/shard_map/fqhd,fkhd->fhqk/dot_general | solution.py:141
  121.3 1.0 reshape.331
  122.3 3.2 fusion.51
  125.5 1.3 copy.104
  126.8 2.8 copy.107
  129.6 1.2 convolution_bitcast_fusion.5
  130.8 1.7 fusion.73
  132.5 1.2 fusion.76
  133.8 5.7 %fusion.6 = bf16[8,20,16,144]{3,2,1,0:T(8,128)(2,1)S(1)} fusion(f32[8,20,16,48]{3,2,1,0:T(8,128)} %fusion.66, f32[8,20,16,48]{3,2,1,0:T(8,128)} %fusion.63, f32[8,20,16,48]{3,2,1,0:T(8,128)} %fusion.60, f32[8,20,16]{2,1,0:T(8,128)S(1)} %copy.108, f32[8,20,16]{2,1,0:T(8,128)S(1)} %fusion.104, pred[8,144]{1,0:T(8,128)(4,1)S(1)} %broadcast_in_dim.62, ...), kind=kLoop, calls=%fused_computation.28 | loop fusion | flops 3686400 | bytes 3708032 | tf_op jit(solution)/shard_map/convert_element_type | solution.py:151
  140.2 1.5 multiply_bitcast_fusion.1
  141.7 1.5 multiply_bitcast_fusion
  143.2 2.6 convolution_bitcast_fusion.2
  145.8 1.5 convolution_bitcast_fusion.1
  147.3 1.5 convolution_bitcast_fusion
  149.2 0.9 pad_maximum_fusion.1
  150.0 5.1 %copy_bitcast_fusion.4 = (f32[8,48,2560]{2,1,0:T(8,128)S(1)}, f32[8,48,2560]{2,1,0:T(8,128)}) fusion(f32[8,20,6,8,128]{4,3,2,1,0:T(8,128)} %convolution_bitcast_fusion.2, f32[8,20,6,8,128]{4,3,2,1,0:T(8,128)S(1)} %multiply_bitcast_fusion.2), kind=kLoop, calls=%fused_computation.16 | loop fusion | bytes 15728640 | tf_op jit(solution)/shard_map/reshape | solution.py:184
  155.1 4.1 %copy_bitcast_fusion.2 = (f32[8,48,2560]{2,1,0:T(8,128)}, f32[8,48,2560]{2,1,0:T(8,128)}) fusion(f32[8,20,6,8,128]{4,3,2,1,0:T(8,128)S(1)} %convolution_bitcast_fusion.1, f32[8,20,6,8,128]{4,3,2,1,0:T(8,128)S(1)} %multiply_bitcast_fusion.1), kind=kLoop, calls=%fused_computation.14 | loop fusion | bytes 15728640 | tf_op jit(solution)/shard_map/reshape | solution.py:184
  159.2 4.1 %copy_bitcast_fusion = (f32[8,48,2560]{2,1,0:T(8,128)}, f32[8,48,2560]{2,1,0:T(8,128)}) fusion(f32[8,20,6,8,128]{4,3,2,1,0:T(8,128)S(1)} %convolution_bitcast_fusion, f32[8,20,6,8,128]{4,3,2,1,0:T(8,128)S(1)} %multiply_bitcast_fusion), kind=kLoop, calls=%fused_computation.12 | loop fusion | bytes 15728640 | tf_op jit(solution)/shard_map/reshape | solution.py:184
  163.3 7.3 %fusion = f32[10,48,5120]{2,1,0:T(8,128)S(1)} fusion(f32[8,48,2560]{2,1,0:T(8,128)} %get-tuple-element.55, f32[8,48,2560]{2,1,0:T(8,128)} %get-tuple-element.56, f32[8,48,2560]{2,1,0:T(8,128)} %get-tuple-element.57, f32[8,48,2560]{2,1,0:T(8,128)} %get-tuple-element.58, f32[8,48,2560]{2,1,0:T(8,128)S(1)} %get-tuple-element.59, f32[8,48,2560]{2,1,0:T(8,128)} %get-tuple-element.60), kind=kLoop, calls=%fused_computation.4 | loop fusion | flops 39321600 | bytes 33423360 | tf_op jit(solution)/shard_map/add | solution.py:189
  171.4 3.0 copy-done.2
  174.4 1.9 slice_bitcast_fusion.3
  176.3 4.3 %collective-permute-start.4 = (bf16[10,16,5120]{2,1,0:T(8,128)(2,1)}, bf16[10,16,5120]{2,1,0:T(8,128)(2,1)}, u32[]{:S(2)}, u32[]{:S(2)}) collective-permute-start(bf16[10,16,5120]{2,1,0:T(8,128)(2,1)} %get-tuple-element.35), channel_id=1, source_target_pairs={{0,1},{1,2},{2,3},{3,4},{4,5},{5,6},{6,7},{7,8},{8,9},{9,10},{10,1... | collective-permute-start | bytes 4915208 | tf_op jit(solution)/shard_map/ppermute | solution.py:14
  180.6 8.0 %collective-permute-start.5 = (bf16[10,16,5120]{2,1,0:T(8,128)(2,1)}, bf16[10,16,5120]{2,1,0:T(8,128)(2,1)}, u32[]{:S(2)}, u32[]{:S(2)}) collective-permute-start(bf16[10,16,5120]{2,1,0:T(8,128)(2,1)} %get-tuple-element.36), channel_id=1, source_target_pairs={{1,0},{2,1},{3,2},{4,3},{5,4},{6,5},{7,6},{8,7},{9,8},{10,9},{11,1... | collective-permute-start | bytes 4915208 | tf_op jit(solution)/shard_map/ppermute | solution.py:14
  188.6 137.4 %all-reduce.5 = bf16[32,5120]{1,0:T(8,128)(2,1)S(1)} all-reduce(f32[32,5120]{1,0:T(8,128)S(1)} %copy-done.19), channel_id=2, replica_groups=mesh['ta'=8,'ha'=64] {'ta','ha'}, use_global_device_ids=true, to_apply=%region_3.4.clone | all-reduce | flops 163840 | bytes 983040
  326.8 2.5 fusion.24
  330.0 0.9 copy-done.9
  333.4 1.2 reshape.335
  334.6 3.6 fusion.122
  338.3 9.7 %collective-permute-start.7 = (bf16[1,16,5120]{2,1,0:T(8,128)(2,1)S(1)}, bf16[1,16,5120]{2,1,0:T(8,128)(2,1)S(1)}, u32[]{:S(2)}, u32[]{:S(2)}) collective-permute-start(bf16[1,16,5120]{2,1,0:T(8,128)(2,1)S(1)} %get-tuple-element.43), channel_id=1, source_target_pairs={{64,0},{128,64},{192,128},{256,192},{320,256},{384,320},{448,384},... | collective-permute-start | bytes 491528 | tf_op jit(solution)/shard_map/ppermute | solution.py:14
  348.1 1.9 collective-permute-start.6
  350.2 27.1 %collective-permute-done.6 = bf16[1,16,5120]{2,1,0:T(8,128)(2,1)S(1)} collective-permute-done((bf16[1,16,5120]{2,1,0:T(8,128)(2,1)S(1)}, bf16[1,16,5120]{2,1,0:T(8,128)(2,1)S(1)}, u32[]{:S(2)}, u32[]{:S(2)}) %collective-permute-start.6) | collective-permute-done | bytes 163872 | tf_op jit(solution)/shard_map/ppermute | solution.py:14
  377.3 1.2 convert_element_type.65
  (99 shorter events, 12.3 us)
Async XLA Ops:
  0.6 6.5 %copy-start = (s32[64,64,2]{1,2,0:T(2,128)S(1)}, s32[64,64,2]{1,2,0:T(2,128)}, u32[]{:S(2)}) copy-start(s32[64,64,2]{1,2,0:T(2,128)} %param.14) | copy-start | bytes 98308
  0.6 40.8 %copy-start.17 = (bf16[8,1,16,2560]{3,2,1,0:T(8,128)(2,1)S(1)}, bf16[8,1,16,2560]{3,2,1,0:T(8,128)(2,1)}, u32[]{:S(2)}) copy-start(bf16[8,1,16,2560]{3,2,1,0:T(8,128)(2,1)} %param.10) | copy-start | bytes 1966084
  1.7 22.9 %collective-permute-start.1 = (bf16[1,1,16,5120]{3,2,1,0:T(8,128)(2,1)S(1)}, bf16[1,1,16,5120]{3,2,1,0:T(8,128)(2,1)S(1)}, u32[]{:S(2)}, u32[]{:S(2)}) collective-permute-start(bf16[1,1,16,5120]{3,2,1,0:T(8,128)(2,1)S(1)} %get-tuple-element.45), channel_id=1, source_target_pairs={{64,0},{128,64},{192,128},{256,192},{320,256},{384,320},{448,384},... | collective-permute-start | bytes 491528 | tf_op jit(solution)/shard_map/ppermute | solution.py:29
  3.7 17.8 %collective-permute-start = (bf16[1,1,16,5120]{3,2,1,0:T(8,128)(2,1)S(1)}, bf16[1,1,16,5120]{3,2,1,0:T(8,128)(2,1)S(1)}, u32[]{:S(2)}, u32[]{:S(2)}) collective-permute-start(bf16[1,1,16,5120]{3,2,1,0:T(8,128)(2,1)S(1)} %get-tuple-element.46), channel_id=1, source_target_pairs={{0,64},{64,128},{128,192},{192,256},{256,320},{320,384},{384,448},... | collective-permute-start | bytes 491528 | tf_op jit(solution)/shard_map/ppermute | solution.py:26
  22.1 21.1 %copy-start.18 = (bf16[8,1,16,2560]{3,2,1,0:T(8,128)(2,1)S(1)}, bf16[8,1,16,2560]{3,2,1,0:T(8,128)(2,1)}, u32[]{:S(2)}) copy-start(bf16[8,1,16,2560]{3,2,1,0:T(8,128)(2,1)} %param.12) | copy-start | bytes 1966084
  25.3 32.1 %collective-permute-start.3 = (bf16[10,1,16,5120]{3,2,1,0:T(8,128)(2,1)}, bf16[10,1,16,5120]{3,2,1,0:T(8,128)(2,1)}, u32[]{:S(2)}, u32[]{:S(2)}) collective-permute-start(bf16[10,1,16,5120]{3,2,1,0:T(8,128)(2,1)} %constant_dynamic-update-slice_fusion), channel_id=1, source_target_pairs={{1,0},{2,1},{3,2},{4,3},{5,4},{6,5},{7,6},{8,7},{9,8},{10,9},{11,1... | collective-permute-start | bytes 4915208 | tf_op jit(solution)/shard_map/ppermute | solution.py:29
  39.5 20.3 %collective-permute-start.2 = (bf16[10,1,16,5120]{3,2,1,0:T(8,128)(2,1)}, bf16[10,1,16,5120]{3,2,1,0:T(8,128)(2,1)}, u32[]{:S(2)}, u32[]{:S(2)}) collective-permute-start(bf16[10,1,16,5120]{3,2,1,0:T(8,128)(2,1)} %constant_dynamic-update-slice_fusion), channel_id=1, source_target_pairs={{0,1},{1,2},{2,3},{3,4},{4,5},{5,6},{6,7},{7,8},{8,9},{9,10},{10,1... | collective-permute-start | bytes 4915208 | tf_op jit(solution)/shard_map/ppermute | solution.py:26
  47.4 15.4 %copy-start.24 = (bf16[4,20,8,128]{3,2,1,0:T(8,128)(2,1)}, bf16[4,20,8,128]{3,2,1,0:T(8,128)(2,1)S(1)}, u32[]{:S(2)}) copy-start(bf16[4,20,8,128]{3,2,1,0:T(8,128)(2,1)S(1)} %get-tuple-element.48) | copy-start | bytes 491524
  47.4 83.4 %copy-start.20 = (bf16[4,20,8,128]{3,2,1,0:T(8,128)(2,1)}, bf16[4,20,8,128]{3,2,1,0:T(8,128)(2,1)S(1)}, u32[]{:S(2)}) copy-start(bf16[4,20,8,128]{3,2,1,0:T(8,128)(2,1)S(1)} %get-tuple-element.47) | copy-start | bytes 491524
  80.4 4.0 %copy-start.13 = (bf16[8,48,20,128]{3,2,1,0:T(8,128)(2,1)S(1)}, bf16[8,48,20,128]{3,2,1,0:T(8,128)(2,1)}, u32[]{:S(2)}) copy-start(bf16[8,48,20,128]{3,2,1,0:T(8,128)(2,1)} %slice.191) | copy-start | bytes 5898244
  90.9 2.9 copy-start.10
  93.9 12.0 %copy-start.3 = (f32[8,20,16,48]{3,2,1,0:T(8,128)}, f32[8,20,16,48]{3,2,1,0:T(8,128)S(1)}, u32[]{:S(2)}) copy-start(f32[8,20,16,48]{3,2,1,0:T(8,128)S(1)} %fusion.69) | copy-start | bytes 1474564
  100.5 2.9 copy-start.4
  103.4 4.5 %copy-start.5 = (f32[8,20,16,48]{3,2,1,0:T(8,128)}, f32[8,20,16,48]{3,2,1,0:T(8,128)S(1)}, u32[]{:S(2)}) copy-start(f32[8,20,16,48]{3,2,1,0:T(8,128)S(1)} %fusion.54) | copy-start | bytes 1474564
  103.4 2.4 copy-start.26
  105.2 0.6 copy-start.22
  105.8 2.1 copy-start.12
  107.9 4.4 %copy-start.6 = (bf16[8,20,16,144]{3,2,1,0:T(8,128)(2,1)}, bf16[8,20,16,144]{3,2,1,0:T(8,128)(2,1)S(1)}, u32[]{:S(2)}) copy-start(bf16[8,20,16,144]{3,2,1,0:T(8,128)(2,1)S(1)} %fusion.7) | copy-start | bytes 2211844
  107.9 2.6 copy-start.14
  116.7 4.0 %copy-start.23 = (f32[8,20,16]{2,1,0:T(8,128)S(1)}, f32[8,20,16]{2,1,0:T(8,128)}, u32[]{:S(2)}) copy-start(f32[8,20,16]{2,1,0:T(8,128)} %copy-done.22) | copy-start | bytes 30724
  116.7 5.6 %copy-start.7 = (bf16[8,20,16,144]{3,2,1,0:T(8,128)(2,1)S(1)}, bf16[8,20,16,144]{3,2,1,0:T(8,128)(2,1)}, u32[]{:S(2)}) copy-start(bf16[8,20,16,144]{3,2,1,0:T(8,128)(2,1)} %copy-done.6) | copy-start | bytes 2211844
  125.5 4.1 %copy-start.15 = (bf16[128,20,128]{0,2,1:T(8,128)(2,1)S(1)}, bf16[128,20,128]{0,2,1:T(8,128)(2,1)}, u32[]{:S(2)}) copy-start(bf16[128,20,128]{0,2,1:T(8,128)(2,1)} %copy.100) | copy-start | bytes 1966084
  141.7 1.5 copy-start.8
  147.3 1.5 copy-start.16
  147.3 1.8 copy-start.21
  170.6 3.8 copy-start.2
  174.4 14.2 %copy-start.19 = (f32[32,5120]{1,0:T(8,128)S(1)}, f32[32,5120]{1,0:T(8,128)}, u32[]{:S(2)}) copy-start(f32[32,5120]{1,0:T(8,128)} %pad_maximum_fusion.1) | copy-start | bytes 1966084
  176.3 158.3 %collective-permute-start.4 = (bf16[10,16,5120]{2,1,0:T(8,128)(2,1)}, bf16[10,16,5120]{2,1,0:T(8,128)(2,1)}, u32[]{:S(2)}, u32[]{:S(2)}) collective-permute-start(bf16[10,16,5120]{2,1,0:T(8,128)(2,1)} %get-tuple-element.35), channel_id=1, source_target_pairs={{0,1},{1,2},{2,3},{3,4},{4,5},{5,6},{6,7},{7,8},{8,9},{9,10},{10,1... | collective-permute-start | bytes 4915208 | tf_op jit(solution)/shard_map/ppermute | solution.py:14
  180.6 154.1 %collective-permute-start.5 = (bf16[10,16,5120]{2,1,0:T(8,128)(2,1)}, bf16[10,16,5120]{2,1,0:T(8,128)(2,1)}, u32[]{:S(2)}, u32[]{:S(2)}) collective-permute-start(bf16[10,16,5120]{2,1,0:T(8,128)(2,1)} %get-tuple-element.36), channel_id=1, source_target_pairs={{1,0},{2,1},{3,2},{4,3},{5,4},{6,5},{7,6},{8,7},{9,8},{10,9},{11,1... | collective-permute-start | bytes 4915208 | tf_op jit(solution)/shard_map/ppermute | solution.py:14
  326.8 2.5 copy-start.11
  329.3 1.7 copy-start.9
  331.7 0.9 copy-start.25
  338.3 38.9 %collective-permute-start.7 = (bf16[1,16,5120]{2,1,0:T(8,128)(2,1)S(1)}, bf16[1,16,5120]{2,1,0:T(8,128)(2,1)S(1)}, u32[]{:S(2)}, u32[]{:S(2)}) collective-permute-start(bf16[1,16,5120]{2,1,0:T(8,128)(2,1)S(1)} %get-tuple-element.43), channel_id=1, source_target_pairs={{64,0},{128,64},{192,128},{256,192},{320,256},{384,320},{448,384},... | collective-permute-start | bytes 491528 | tf_op jit(solution)/shard_map/ppermute | solution.py:14
  348.1 29.2 %collective-permute-start.6 = (bf16[1,16,5120]{2,1,0:T(8,128)(2,1)S(1)}, bf16[1,16,5120]{2,1,0:T(8,128)(2,1)S(1)}, u32[]{:S(2)}, u32[]{:S(2)}) collective-permute-start(bf16[1,16,5120]{2,1,0:T(8,128)(2,1)S(1)} %get-tuple-element.44), channel_id=1, source_target_pairs={{0,64},{64,128},{128,192},{192,256},{256,320},{320,384},{384,448},... | collective-permute-start | bytes 491528 | tf_op jit(solution)/shard_map/ppermute | solution.py:14
  377.2 1.3 copy-start.1
where the time goes:
time: 380 us; the launch traced here: 379 us
  blocking collectives  137 us (36%)
  local copies, waits for them, and re-layouts  73.4 us (19%)
  waiting for transfers between devices  50 us (13%)
  starting transfers between devices  45.3 us (12%)
  matrix products  44.6 us (12%)
  other arithmetic  26.6 us (7%)
    unnamed x1, blocking collectives  137 us
    ppermute x4, waiting for transfers between devices, passed_along(): return lax.ppermute(block, axis, route)  27.1 us
    ppermute x4, starting transfers between devices, passed_along(): return lax.ppermute(block, axis, route)  23.9 us
    slice x4, local copies, waits for them, and re-layouts, on_device(): keys_ext[step:step + frames_dev]  17.6 us
    ppermute x2, waiting for transfers between devices, padded(): lax.ppermute(lax.slice_in_dim(block, block.shape[dim] - width, None, axis...  16.6 us
    ppermute x2, starting transfers between devices, padded(): lax.ppermute(lax.slice_in_dim(block, 0, width, axis=dim), axis, backward)  16.1 us
    reshape x3, local copies, waits for them, and re-layouts, on_device(): value_part.reshape(frames_dev, band, feature_width)  13.3 us
    slice x3, local copies, waits for them, and re-layouts, on_device(): values_ext[step:step + frames_dev]  13 us
  transfers between devices with their start and end apart: 8, of which 4 were waited for; matrix products, arithmetic and copies ran while one was open for 5% of the time, Pallas kernels for 0%

commit v1 on v0

v1 whole, which is shorter than its diff:
```python
import functools
import math

import jax
import jax.numpy as jnp
from jax import lax
from jax.experimental import pallas as pl
from jax.experimental.pallas import tpu as pltpu
from jax.sharding import PartitionSpec as P

HD = 128
MESH = pl.DeviceIdType.MESH
F32 = jnp.float32
BF16 = jnp.bfloat16

HEADS_PER_GROUP = 2
AHEAD = 2
LAG_TOTALS = 1
LAG_GRADS = 2
LAG_FOLD = 4


def both_last(a, b):
    return lax.dot_general(a, b, (((1,), (1,)), ((), ())), preferred_element_type=F32)


def both_first(a, b):
    return lax.dot_general(a, b, (((0,), (0,)), ((), ())), preferred_element_type=F32)


def plain(a, b):
    return lax.dot_general(a, b, (((1,), (0,)), ((), ())), preferred_element_type=F32)


def attention_kernel(
    nt,
    nh,
    q_hbm,
    kv_hbm,
    do_hbm,
    text,
    lanes,
    dq_out,
    dkv_out,
    text_out,
    q_all,
    do_all,
    kv_all,
    bias,
    e_all,
    dp_all,
    stat_send,
    stat_recv,
    stat_own,
    coef_recv,
    coef_own,
    dq_send,
    dq_recv,
    dq_own,
    dkv_send,
    dkv_recv,
    dkv_own,
    own_sem,
    row_s,
    row_r,
    fr_s,
    fr_r,
    stat_s,
    stat_r,
    coef_s,
    coef_r,
    dq_s,
    dq_r,
    dkv_s,
    dkv_r,
):
    frames, columns = q_all.shape[1], q_all.shape[2]
    width = q_all.shape[3]
    tokens = frames * columns
    texts = text.shape[0]
    heads = width // HD
    hg = HEADS_PER_GROUP
    groups = heads // hg
    gw = hg * HD
    scale = 1.0 / math.sqrt(HD)
    keys = texts + (frames + 2) * columns
    ta, ha = lax.axis_index("ta"), lax.axis_index("ha")
    has_dn, has_up = ha > 0, ha < nh - 1
    has_prev, has_next = ta > 0, ta < nt - 1
    dn, up = {"ha": ha - 1}, {"ha": ha + 1}
    prev, nxt = {"ta": ta - 1}, {"ta": ta + 1}

    own_copies = [
        pltpu.make_async_copy(q_hbm.at[:, 0], q_all.at[1], own_sem.at[0]),
        pltpu.make_async_copy(do_hbm.at[:, 0], do_all.at[1], own_sem.at[1]),
        pltpu.make_async_copy(kv_hbm.at[:, 0], kv_all.at[pl.ds(1, frames)], own_sem.at[2]),
    ]
    for copy in own_copies:
        copy.start()

    barrier = pltpu.get_barrier_semaphore()
    sides = ((has_dn, dn), (has_up, up), (has_prev, prev), (has_next, nxt))
    for has, where in sides:

        @pl.when(has)
        def _(where=where):
            pl.semaphore_signal(barrier, inc=1, device_id=where, device_id_type=MESH)

    pl.semaphore_wait(barrier, sum(has.astype(jnp.int32) for has, _ in sides))

    def at(g, base=0):
        return pl.ds(pl.multiple_of(base + g * gw, HD), gw)

    def remote(src, dst, send, recv, where):
        return pltpu.make_async_remote_copy(
            src_ref=src,
            dst_ref=dst,
            send_sem=send,
            recv_sem=recv,
            device_id=where,
            device_id_type=MESH,
        )

    def row_copies(g, side, where):
        slot = 0 if side == 0 else 2
        return [
            remote(q_hbm.at[:, 0, :, at(g)], q_all.at[slot, :, :, at(g)], row_s.at[side, 0, g], row_r.at[side, 0, g], where),
            remote(do_hbm.at[:, 0, :, at(g)], do_all.at[slot, :, :, at(g)], row_s.at[side, 1, g], row_r.at[side, 1, g], where),
        ]

    def frame_copies(g, side, where):
        source = frames - 1 if side == 0 else 0
        slot = 0 if side == 0 else frames + 1
        return [
            remote(
                kv_hbm.at[source, 0, :, at(g, base)],
                kv_all.at[slot, :, at(g, base)],
                fr_s.at[side, i, g],
                fr_r.at[side, i, g],
                where,
            )
            for i, base in enumerate((0, width))
        ]

    def stat_copy(g, side, where):
        return remote(stat_send.at[side, g], stat_recv.at[side, g], stat_s.at[side, g], stat_r.at[side, g], where)

    def coef_copy(g, side, where):
        return remote(coef_own.at[g], coef_recv.at[side, g], coef_s.at[side, g], coef_r.at[side, g], where)

    def dq_copy(g, side, where):
        return remote(
            dq_send.at[side, :, :, at(g)], dq_recv.at[side, :, :, at(g)], dq_s.at[side, g], dq_r.at[side, g], where
        )

    def dkv_copies(g, side, where):
        return [
            remote(
                dkv_send.at[side, :, at(g, base)],
                dkv_recv.at[side, :, at(g, base)],
                dkv_s.at[side, i, g],
                dkv_r.at[side, i, g],
                where,
            )
            for i, base in enumerate((0, width))
        ]

    row_routes = ((0, has_up, up, has_dn), (1, has_dn, dn, has_up))
    frame_routes = ((0, has_next, nxt, has_prev), (1, has_prev, prev, has_next))

    def as_list(x):
        return x if isinstance(x, list) else [x]

    def start(make, routes, g):
        for side, has, where, _ in routes:

            @pl.when(has)
            def _(side=side, where=where):
                for copy in as_list(make(g, side, where)):
                    copy.start()

    def arrived(make, routes, g):
        for side, _, where, has in routes:

            @pl.when(has)
            def _(side=side, where=where):
                for copy in as_list(make(g, side, where)):
                    copy.wait_recv()

    def sent(make, routes, g):
        for side, has, where, _ in routes:

            @pl.when(has)
            def _(side=side, where=where):
                for copy in as_list(make(g, side, where)):
                    copy.wait_send()

    def forward(g):
        start(frame_copies, frame_routes, g)
        start(row_copies, row_routes, g)

    for g in range(min(AHEAD, groups)):
        forward(g)

    for side, _, _, has in row_routes:

        @pl.when(jnp.logical_not(has))
        def _(side=side):
            slot = 0 if side == 0 else 2
            q_all[slot] = jnp.zeros(q_all.shape[1:], BF16)
            do_all[slot] = jnp.zeros(do_all.shape[1:], BF16)
            stat_recv[side] = jnp.zeros(stat_recv.shape[1:], F32)
            coef_recv[side] = jnp.zeros(coef_recv.shape[1:], F32)
            dq_recv[side] = jnp.zeros(dq_recv.shape[1:], BF16)

    for side, _, _, has in frame_routes:

        @pl.when(jnp.logical_not(has))
        def _(side=side):
            slot = 0 if side == 0 else frames + 1
            kv_all[slot] = jnp.zeros(kv_all.shape[1:], BF16)
            dkv_recv[side] = jnp.zeros(dkv_recv.shape[1:], BF16)

    line = lax.broadcasted_iota(jnp.int32, (keys, 3 * tokens), 0)
    lane = lax.broadcasted_iota(jnp.int32, (keys, 3 * tokens), 1)
    query_frame = lax.rem(lane, tokens) // columns
    key_frame = (line - texts + columns) // columns - 2
    gap = jnp.abs(key_frame - query_frame)
    inside = ((key_frame >= 0) | has_prev) & ((key_frame < frames) | has_next)
    latent_seen = (line >= texts) & inside & (gap <= lanes[0:1, :])
    text_seen = (line < texts) & (line < lanes[1:2, :])
    bias[...] = jnp.where(latent_seen | text_seen, 0.0, -1e30)
    for copy in own_copies:
        copy.wait()

    def operands(h):
        cols = pl.ds(pl.multiple_of(h * HD, HD), HD)
        vcols = pl.ds(pl.multiple_of(width + h * HD, HD), HD)
        q3 = q_all[:, :, :, cols].reshape(3 * tokens, HD)
        do3 = do_all[:, :, :, cols].reshape(3 * tokens, HD)
        kall = jnp.concatenate([text[:, cols], kv_all[:, :, cols].reshape(-1, HD)], axis=0)
        vall = jnp.concatenate([text[:, vcols], kv_all[:, :, vcols].reshape(-1, HD)], axis=0)
        return q3, do3, kall, vall, cols, vcols

    def scores(g):
        arrived(frame_copies, frame_routes, g)
        arrived(row_copies, row_routes, g)
        sums = []
        for i in range(hg):
            h = g * hg + i
            q3, do3, kall, vall, _, _ = operands(h)
            s = both_last(kall, q3)
            dp = both_last(vall, do3)
            e = jnp.exp(s * scale + bias[...])
            e_all[h] = e
            dp_all[h] = dp
            sums.append((jnp.sum(e, axis=0, keepdims=True), jnp.sum(e * dp, axis=0, keepdims=True)))
        filler = [jnp.ones((1, tokens), F32)] * (4 - hg)
        for part, (ref, index) in enumerate(((stat_send, (1, g)), (stat_own, (g,)), (stat_send, (0, g)))):
            cut = slice(part * tokens, (part + 1) * tokens)
            lines = [a[:, cut] for a, _ in sums] + filler + [b[:, cut] for _, b in sums] + filler
            ref[index] = jnp.concatenate(lines, axis=0)
        start(stat_copy, row_routes, g)

    def totals(g):
        arrived(stat_copy, row_routes, g)
        total = stat_own[g] + stat_recv[0, g] + stat_recv[1, g]
        inverse = 1.0 / total[0:4]
        coef_own[g] = jnp.concatenate([inverse, total[4:8] * inverse], axis=0)
        start(coef_copy, row_routes, g)

    def grads(g):
        arrived(coef_copy, row_routes, g)
        coef = jnp.concatenate([coef_recv[0, g], coef_own[g], coef_recv[1, g]], axis=1)
        for i in range(hg):
            h = g * hg + i
            q3, do3, kall, _, cols, vcols = operands(h)
            p = e_all[h] * coef[i : i + 1]
            half = p.astype(BF16)
            ds = (p * (dp_all[h] - coef[4 + i : 5 + i])).astype(BF16)
            dv = plain(half, do3)
            dk = plain(ds, q3) * scale
            dq = both_first(ds, kall) * scale
            for grad, where in ((dk, cols), (dv, vcols)):
                text_out[:, where] = grad[0:texts]
                dkv_send[1, :, where] = grad[texts : texts + columns].astype(BF16)
                dkv_own[:, :, where] = grad[texts + columns : texts + columns + tokens].reshape(frames, columns, HD)
                dkv_send[0, :, where] = grad[texts + columns + tokens :].astype(BF16)
            dq_send[1, :, :, cols] = dq[0:tokens].astype(BF16).reshape(frames, columns, HD)
            dq_own[:, :, cols] = dq[tokens : 2 * tokens].reshape(frames, columns, HD)
            dq_send[0, :, :, cols] = dq[2 * tokens :].astype(BF16).reshape(frames, columns, HD)
        start(dkv_copies, frame_routes, g)
        start(dq_copy, row_routes, g)

    def fold(g):
        arrived(dkv_copies, frame_routes, g)
        arrived(dq_copy, row_routes, g)
        cols = at(g)
        total = dq_own[:, :, cols] + dq_recv[0, :, :, cols].astype(F32) + dq_recv[1, :, :, cols].astype(F32)
        dq_out[:, 0, :, cols] = total.astype(BF16)
        for base in (0, width):
            where = at(g, base)
            dkv_out[0, 0, :, where] = (dkv_own[0, :, where] + dkv_recv[0, :, where].astype(F32)).astype(BF16)
            dkv_out[1 : frames - 1, 0, :, where] = dkv_own[1 : frames - 1, :, where].astype(BF16)
            dkv_out[frames - 1, 0, :, where] = (
                dkv_own[frames - 1, :, where] + dkv_recv[1, :, where].astype(F32)
            ).astype(BF16)

    def step(s, carry):
        for lag, stage in ((-AHEAD, forward), (0, scores), (LAG_TOTALS, totals), (LAG_GRADS, grads), (LAG_FOLD, fold)):

            @pl.when((s >= max(lag, 0)) & (s < groups + lag))
            def _(lag=lag, stage=stage):
                stage(s - lag)

        return carry

    lax.fori_loop(0, groups + LAG_FOLD, step, 0)

    def drain(g, carry):
        for make, routes in (
            (frame_copies, frame_routes),
            (row_copies, row_routes),
            (stat_copy, row_routes),
            (coef_copy, row_routes),
            (dkv_copies, frame_routes),
            (dq_copy, row_routes),
        ):
            sent(make, routes, g)
        return carry

    lax.fori_loop(0, groups, drain, 0)


def attention_grads(nt, nh, query, key_value, out_grad, text_kv, lanes):
    frames, _, columns, width = query.shape
    tokens = frames * columns
    texts = text_kv.shape[0]
    heads = width // HD
    groups = heads // HEADS_PER_GROUP
    keys = texts + (frames + 2) * columns
    dma = pltpu.SemaphoreType.DMA
    here = pl.BlockSpec(memory_space=pltpu.VMEM)
    away = pl.BlockSpec(memory_space=pl.ANY)
    return pl.pallas_call(
        functools.partial(attention_kernel, nt, nh),
        out_shape=(
            jax.ShapeDtypeStruct(query.shape, BF16),
            jax.ShapeDtypeStruct(key_value.shape, BF16),
            jax.ShapeDtypeStruct((texts, 2 * width), F32),
        ),
        in_specs=[away, away, away, here, here],
        out_specs=(here, here, here),
        scratch_shapes=[
            pltpu.VMEM((3, frames, columns, width), BF16),
            pltpu.VMEM((3, frames, columns, width), BF16),
            pltpu.VMEM((frames + 2, columns, 2 * width), BF16),
            pltpu.VMEM((keys, 3 * tokens), F32),
            pltpu.VMEM((heads, keys, 3 * tokens), F32),
            pltpu.VMEM((heads, keys, 3 * tokens), F32),
            pltpu.VMEM((2, groups, 8, tokens), F32),
            pltpu.VMEM((2, groups, 8, tokens), F32),
            pltpu.VMEM((groups, 8, tokens), F32),
            pltpu.VMEM((2, groups, 8, tokens), F32),
            pltpu.VMEM((groups, 8, tokens), F32),
            pltpu.VMEM((2, frames, columns, width), BF16),
            pltpu.VMEM((2, frames, columns, width), BF16),
            pltpu.VMEM((frames, columns, width), F32),
            pltpu.VMEM((2, columns, 2 * width), BF16),
            pltpu.VMEM((2, columns, 2 * width), BF16),
            pltpu.VMEM((frames, columns, 2 * width), F32),
            dma((3,)),
            dma((2, 2, groups)),
            dma((2, 2, groups)),
            dma((2, 2, groups)),
            dma((2, 2, groups)),
            dma((2, groups)),
            dma((2, groups)),
            dma((2, groups)),
            dma((2, groups)),
            dma((2, groups)),
            dma((2, groups)),
            dma((2, 2, groups)),
            dma((2, 2, groups)),
        ],
        compiler_params=pltpu.CompilerParams(collective_id=0, has_side_effects=True, vmem_limit_bytes=60 << 20),
        name="attention_grads",
    )(query, key_value, out_grad, text_kv, lanes)


def lane_limits(tile_reach, text_len, frames, columns):
    time_index, row_index = lax.axis_index("ta"), lax.axis_index("ha")
    first = time_index * frames
    padded = jnp.pad(tile_reach, ((0, 0), (1, 1), (0, 0)), constant_values=-1)
    near = lax.dynamic_slice(padded, (first, row_index, 0), (frames, 3, 2))
    away = jnp.abs(jnp.arange(3, dtype=jnp.int32) - 1)[None, :]
    reach = jnp.where(near[..., 1] >= away, near[..., 0], -1)
    reach = jnp.repeat(reach.T.reshape(-1), columns)
    length = lax.dynamic_slice(text_len, (first, row_index), (frames, 1))[:, 0]
    length = jnp.repeat(jnp.pad(length, (frames, frames)), columns)
    return jnp.stack([reach, length])


def on_device(nt, nh, query, key_value, out_grad, text_kv, tile_reach, text_len):
    lanes = lane_limits(tile_reach, text_len, query.shape[0], query.shape[2])
    query_grad, key_value_grad, text_partial = attention_grads(nt, nh, query, key_value, out_grad, text_kv, lanes)
    text_grad = lax.psum_scatter(text_partial, ("ta", "ha"), scatter_dimension=1, tiled=True).astype(BF16)
    return query_grad, key_value_grad, text_grad


def solution(mesh):
    placed = (
        P("ta", "ha", None, None),
        P("ta", "ha", None, None),
        P("ta", "ha", None, None),
        P(),
        P(),
        P(),
    )
    return jax.shard_map(
        functools.partial(on_device, mesh.shape["ta"], mesh.shape["ha"]),
        mesh=mesh,
        in_specs=placed,
        out_specs=(P("ta", "ha", None, None), P("ta", "ha", None, None), P(None, ("ta", "ha"))),
        check_vma=False,
    )
```

time: 380 us -> 216 us (0.57)
  the two profiles are of different devices: /device:TPU:289 before, /device:TPU:7 now
where the time goes in v1:
time: 216 us; the launch traced here: 214 us
  blocking collectives  106 us (49%)
  Pallas kernels  101 us (47%)
  local copies, waits for them, and re-layouts  6.23 us (3%)
    unnamed x1, blocking collectives  106 us
    pallas_call x1, Pallas kernels, attention_grads(): pl.pallas_call(functools.partial(attention_kernel, nt, nh), out_shape=(ja...  101 us
    unnamed x7, local copies, waits for them, and re-layouts  4.46 us

profile of v1, /device:TPU:7, one launch (start us, length us, event | category | flops | bytes accessed | tf_op | source)
XLA Modules:
  0.0 213.7 jit_solution(9964991117140499500)
XLA Ops:
  0.6 0.0 copy-start
  0.7 0.7 copy-done
  1.4 0.2 dynamic-slice_reduce_fusion
  1.6 0.1 pad.9
  1.7 0.9 pad_dynamic-slice_fusion
  2.5 0.1 copy.15
  2.6 0.1 copy.16
  2.7 0.1 fusion
  2.8 0.1 reshape.14
  2.9 0.1 broadcast_in_dim.12
  2.9 0.1 stack_reshape.6
  3.0 0.1 broadcast_in_dim.13
  3.1 0.1 stack_reshape.7
  3.2 0.6 pad_add_fusion.lanes
  3.8 100.5 %attention_grads.1 = (bf16[8,1,16,2560]{3,2,1,0:T(8,128)(2,1)}, bf16[8,1,16,5120]{3,2,1,0:T(8,128)(2,1)}, f32[32,5120]{1,0:T(8,128)}) custom-call(bf16[8,1,16,2560]{3,2,1,0:T(8,128)(2,1)} %q_hbm.1, bf16[8,1,16,5120]{3,2,1,0:T(8,128)(2,1)} %kv_hbm.1, bf16[8,1,16,2560]{3,2,1,0:T(8,128)(2,1)} %do_hbm.1, bf16[32,5120]{1,0:T(8,128)(2,1)} %text.1, ...), custom_call_target="tpu_custom_call" | custom-call | tf_op jit(solution)/shard_map/attention_grads/pallas_call | solution.py:345
  104.3 0.0 copy-start.1
  104.3 105.6 %all-reduce.4 = bf16[32,5120]{1,0:T(8,128)(2,1)S(1)} all-reduce(f32[32,5120]{1,0:T(8,128)} %get-tuple-element.8), channel_id=2, replica_groups=mesh['ta'=8,'ha'=64] {'ta','ha'}, use_global_device_ids=true, to_apply=%region_0.1.clone | all-reduce | flops 163840 | bytes 983040
  209.9 0.1 dynamic-slice_convert_fusion
  210.0 0.7 copy.17
  210.7 2.0 copy.24
  212.7 0.0 copy-done.1
  212.7 1.1 copy.25
  (1 shorter events, 0.0 us)
Async XLA Ops:
  0.6 0.8 copy-start
  104.3 108.4 %copy-start.1 = (bf16[8,1,16,5120]{3,2,1,0:T(8,128)(2,1)S(1)}, bf16[8,1,16,5120]{3,2,1,0:T(8,128)(2,1)}, u32[]{:S(2)}) copy-start(bf16[8,1,16,5120]{3,2,1,0:T(8,128)(2,1)} %get-tuple-element.24) | copy-start | bytes 3932164

commit v2 on v1

v2 whole, which is shorter than its diff:
```python
import functools
import math

import jax
import jax.numpy as jnp
from jax import lax
from jax.experimental import pallas as pl
from jax.experimental.pallas import tpu as pltpu
from jax.sharding import PartitionSpec as P

HD = 128
MESH = pl.DeviceIdType.MESH
F32 = jnp.float32
BF16 = jnp.bfloat16

AHEAD = 2
LAG_GRADS = 1
LAG_RELAY = 2
LAG_TEXT = 2
LAG_FOLD = 4
GROUPS = 4
RUN = 8
LINES = 8


def both_last(a, b):
    return lax.dot_general(a, b, (((1,), (1,)), ((), ())), preferred_element_type=F32)


def both_first(a, b):
    return lax.dot_general(a, b, (((0,), (0,)), ((), ())), preferred_element_type=F32)


def plain(a, b):
    return lax.dot_general(a, b, (((1,), (0,)), ((), ())), preferred_element_type=F32)


def attention_kernel(
    nt,
    nh,
    q_hbm,
    kv_hbm,
    do_hbm,
    text,
    lanes,
    dq_out,
    dkv_out,
    text_out,
    q_all,
    do_all,
    kv_all,
    bias,
    e_all,
    dp_all,
    stat_send,
    near_recv,
    far_recv,
    dq_send,
    dq_recv,
    dq_own,
    dkv_send,
    dkv_recv,
    dkv_own,
    relay_kv,
    relay_dkv,
    text_part,
    core_recv,
    x_own,
    x_recv,
    y_own,
    y_recv,
    z_own,
    z_recv,
    all_recv,
    own_sem,
    row_s,
    row_r,
    fr_s,
    fr_r,
    near_s,
    near_r,
    far_s,
    far_r,
    dq_s,
    dq_r,
    dkv_s,
    dkv_r,
    relay_s,
    relay_r,
    core_s,
    core_r,
    x_s,
    x_r,
    y_s,
    y_r,
    z_s,
    z_r,
    all_s,
    all_r,
):
    frames, columns = q_all.shape[1], q_all.shape[2]
    width = q_all.shape[3]
    tokens = frames * columns
    texts = text.shape[0]
    heads = width // HD
    groups = GROUPS
    hg = heads // groups
    gw = hg * HD
    scale = 1.0 / math.sqrt(HD)
    keys = texts + (frames + 2) * columns
    ta, ha = lax.axis_index("ta"), lax.axis_index("ha")
    nx = nt // 2
    ny = nh // (2 * RUN)
    half, x = ta // nx, lax.rem(ta, nx)
    core = lax.rem(ha, 2)
    z = lax.rem(ha // 2, RUN)
    y = ha // (2 * RUN)
    first, last = nx - 1, nx
    has_dn, has_up = ha > 0, ha < nh - 1
    has_dn2, has_up2 = ha > 1, ha < nh - 2
    has_prev, has_next = ta > 0, ta < nt - 1
    dn, up = {"ha": ha - 1}, {"ha": ha + 1}
    dn2, up2 = {"ha": ha - 2}, {"ha": ha + 2}
    prev, nxt = {"ta": ta - 1}, {"ta": ta + 1}
    partner = {"ha": ha + 1 - 2 * core}

    def spot(c, yy, zz):
        return (yy * RUN + zz) * 2 + c

    own_copies = [
        pltpu.make_async_copy(q_hbm.at[:, 0], q_all.at[1], own_sem.at[0]),
        pltpu.make_async_copy(do_hbm.at[:, 0], do_all.at[1], own_sem.at[1]),
        pltpu.make_async_copy(kv_hbm.at[:, 0], kv_all.at[pl.ds(1, frames)], own_sem.at[2]),
    ]
    for copy in own_copies:
        copy.start()

    always = ta >= 0
    x_peers = [lax.rem(x + d, nx) for d in range(1, nx)]
    y_peers = [lax.rem(y + d, ny) for d in range(1, ny)]
    all_peers = [(core, yy) for yy in y_peers] + [(1 - core, lax.rem(y + d, ny)) for d in range(ny)]
    z_here = half * RUN + z
    z_peers = [lax.rem(z_here + d, 2 * RUN) for d in range(1, 2 * RUN)]
    greet = [(has_dn, dn), (has_up, up), (has_dn2, dn2), (has_up2, up2)]
    greet += [(always, {"ta": half * nx + xx}) for xx in x_peers]
    greet += [(always, {"ha": spot(c, yy, z)}) for c, yy in all_peers]
    greet += [(always, {"ta": (p // RUN) * nx + x, "ha": spot(core, y, lax.rem(p, RUN))}) for p in z_peers]
    greet += [(ta == first, {"ta": nx + j}) for j in range(nx)]
    greet += [(ta == last, {"ta": j}) for j in range(nx)]
    greet += [(ta < first, {"ta": last}), (ta > last, {"ta": first})]
    barrier = pltpu.get_barrier_semaphore()
    for has, where in greet:

        @pl.when(has)
        def _(where=where):
            pl.semaphore_signal(barrier, inc=1, device_id=where, device_id_type=MESH)

    pl.semaphore_wait(barrier, sum(has.astype(jnp.int32) for has, _ in greet))

    def at(g, base=0):
        return pl.ds(pl.multiple_of(base + g * gw, HD), gw)

    def remote(src, dst, send, recv, where):
        return pltpu.make_async_remote_copy(
            src_ref=src,
            dst_ref=dst,
            send_sem=send,
            recv_sem=recv,
            device_id=where,
            device_id_type=MESH,
        )

    def row_copies(g, side, where):
        slot = 0 if side == 0 else 2
        return [
            remote(
                hbm.at[:, 0, :, at(g)], ref.at[slot, :, :, at(g)], row_s.at[side, i, g], row_r.at[side, i, g], where
            )
            for i, (hbm, ref) in enumerate(((q_hbm, q_all), (do_hbm, do_all)))
        ]

    bases = (0, width)

    def kv_source(g, side, base):
        return kv_hbm.at[frames - 1 if side == 0 else 0, 0, :, at(g, base)]

    def kv_target(g, side, base):
        return kv_all.at[0 if side == 0 else frames + 1, :, at(g, base)]

    def dkv_source(g, side, base):
        return dkv_send.at[side, :, at(g, base)]

    def dkv_target(g, side, base):
        return dkv_recv.at[side, :, at(g, base)]

    def frame_copies(g, side, where):
        return [
            remote(
                kv_source(g, side, base), kv_target(g, side, base), fr_s.at[side, i, g], fr_r.at[side, i, g], where
            )
            for i, base in enumerate(bases)
        ]

    def dkv_copies(g, side, where):
        return [
            remote(
                dkv_source(g, side, base), dkv_target(g, side, base), dkv_s.at[side, i, g], dkv_r.at[side, i, g], where
            )
            for i, base in enumerate(bases)
        ]

    def to_relay(kind, g, side, where):
        source, send, held = ((kv_source, fr_s, relay_kv), (dkv_source, dkv_s, relay_dkv))[kind]
        return [
            remote(source(g, side, base), held.at[i], send.at[side, i, g], relay_r.at[kind, i], where)
            for i, base in enumerate(bases)
        ]

    def from_relay(kind, g, side, where):
        held, target, recv = ((relay_kv, kv_target, fr_r), (relay_dkv, dkv_target, dkv_r))[kind]
        return [
            remote(held.at[i], target(g, side, base), relay_s.at[kind, i], recv.at[side, i, g], where)
            for i, base in enumerate(bases)
        ]

    def near_copy(g, side, where):
        return [remote(stat_send.at[side, g], near_recv.at[side, g], near_s.at[side, g], near_r.at[side, g], where)]

    def far_copy(g, side, where):
        return [remote(stat_send.at[side, g, 0], far_recv.at[side, g], far_s.at[side, g], far_r.at[side, g], where)]

    def dq_copy(g, side, where):
        return [
            remote(
                dq_send.at[side, :, :, at(g)], dq_recv.at[side, :, :, at(g)], dq_s.at[side, g], dq_r.at[side, g], where
            )
        ]

    row_routes = ((0, has_up, up, has_dn), (1, has_dn, dn, has_up))
    far_routes = ((0, has_up2, up2, has_dn2), (1, has_dn2, dn2, has_up2))
    frame_routes = ((0, has_next, nxt, has_prev), (1, has_prev, prev, has_next))
    crossings = ((0, ta == first, nxt), (1, ta == last, prev))

    def start(make, routes, g):
        for side, has, where, _ in routes:

            @pl.when(has)
            def _(side=side, where=where):
                for copy in make(g, side, where):
                    copy.start()

    def arrived(make, routes, g):
        for side, _, where, has in routes:

            @pl.when(has)
            def _(side=side, where=where):
                for copy in make(g, side, where):
                    copy.wait_recv()

    def sent(make, routes, g):
        for side, has, where, _ in routes:

            @pl.when(has)
            def _(side=side, where=where):
                for copy in make(g, side, where):
                    copy.wait_send()

    def start_frames(kind, g):
        make = (frame_copies, dkv_copies)[kind]
        for (side, has, where, _), (_, crosses, _) in zip(frame_routes, crossings):
            relayed = crosses & (g != x)

            @pl.when(has & jnp.logical_not(relayed))
            def _(side=side, where=where):
                for copy in make(g, side, where):
                    copy.start()

            @pl.when(relayed)
            def _(side=side):
                for copy in to_relay(kind, g, side, {"ta": half * nx + g}):
                    copy.start()

    relays = ((0, (half == 0) & (ta != first), {"ta": last}), (1, (half == 1) & (ta != last), {"ta": first}))

    def pass_on(kind):
        for side, has, where in relays:

            @pl.when(has)
            def _(side=side, where=where):
                for copy in to_relay(kind, x, side, where):
                    copy.wait_recv()
                for copy in from_relay(kind, x, side, where):
                    copy.start()

    def passed_on(kind):
        for side, has, where in relays:

            @pl.when(has)
            def _(side=side, where=where):
                for copy in from_relay(kind, x, side, where):
                    copy.wait_send()

    def forward(g):
        start(row_copies, row_routes, g)

    for g in range(groups):
        start_frames(0, g)
    for g in range(AHEAD):
        forward(g)

    for side, _, _, has in row_routes:

        @pl.when(jnp.logical_not(has))
        def _(side=side):
            slot = 0 if side == 0 else 2
            q_all[slot] = jnp.zeros(q_all.shape[1:], BF16)
            do_all[slot] = jnp.zeros(do_all.shape[1:], BF16)
            near_recv[side, :, 0] = jnp.zeros((groups,) + near_recv.shape[3:], F32)
            near_recv[side, :, 1] = jnp.ones((groups,) + near_recv.shape[3:], F32)
            dq_recv[side] = jnp.zeros(dq_recv.shape[1:], BF16)

    for side, _, _, has in far_routes:

        @pl.when(jnp.logical_not(has))
        def _(side=side):
            far_recv[side] = jnp.zeros(far_recv.shape[1:], F32)

    for side, _, _, has in frame_routes:

        @pl.when(jnp.logical_not(has))
        def _(side=side):
            slot = 0 if side == 0 else frames + 1
            kv_all[slot] = jnp.zeros(kv_all.shape[1:], BF16)
            dkv_recv[side] = jnp.zeros(dkv_recv.shape[1:], BF16)

    line = lax.broadcasted_iota(jnp.int32, (keys, 3 * tokens), 0)
    lane = lax.broadcasted_iota(jnp.int32, (keys, 3 * tokens), 1)
    query_frame = lax.rem(lane, tokens) // columns
    key_frame = (line - texts + columns) // columns - 2
    gap = jnp.abs(key_frame - query_frame)
    inside = ((key_frame >= 0) | has_prev) & ((key_frame < frames) | has_next)
    latent_seen = (line >= texts) & inside & (gap <= lanes[0:1, :])
    text_seen = (line < texts) & (line < lanes[1:2, :])
    bias[...] = jnp.where(latent_seen | text_seen, 0.0, -1e30)
    pass_on(0)
    for copy in own_copies:
        copy.wait()

    def operands(h):
        cols = pl.ds(pl.multiple_of(h * HD, HD), HD)
        vcols = pl.ds(pl.multiple_of(width + h * HD, HD), HD)
        q3 = q_all[:, :, :, cols].reshape(3 * tokens, HD)
        do3 = do_all[:, :, :, cols].reshape(3 * tokens, HD)
        kall = jnp.concatenate([text[:, cols], kv_all[:, :, cols].reshape(-1, HD)], axis=0)
        vall = jnp.concatenate([text[:, vcols], kv_all[:, :, vcols].reshape(-1, HD)], axis=0)
        return q3, do3, kall, vall, cols, vcols

    def scores(g):
        arrived(frame_copies, frame_routes, g)
        arrived(row_copies, row_routes, g)
        sums = []
        for i in range(hg):
            h = g * hg + i
            q3, do3, kall, vall, _, _ = operands(h)
            s = both_last(kall, q3)
            dp = both_last(vall, do3)
            e = jnp.exp(s * scale + bias[...])
            e_all[h] = e
            dp_all[h] = dp
            sums.append((jnp.sum(e, axis=0, keepdims=True), jnp.sum(e * dp, axis=0, keepdims=True)))
        filler = [jnp.ones((1, tokens), F32)] * (LINES - hg)
        blocks = []
        for part in range(3):
            cut = slice(part * tokens, (part + 1) * tokens)
            lines = [a[:, cut] for a, _ in sums] + filler + [b[:, cut] for _, b in sums] + filler
            blocks.append(jnp.concatenate(lines, axis=0))
        stat_send[0, g, 0] = blocks[2]
        stat_send[1, g, 0] = blocks[0]
        stat_send[0, g, 1] = blocks[1]
        stat_send[1, g, 1] = blocks[1]
        start(near_copy, row_routes, g)
        start(far_copy, far_routes, g)

    def grads(g):
        arrived(near_copy, row_routes, g)
        arrived(far_copy, far_routes, g)
        total = jnp.concatenate(
            [
                stat_send[1, g, 0] + near_recv[0, g, 1] + far_recv[0, g],
                stat_send[0, g, 1] + near_recv[0, g, 0] + near_recv[1, g, 0],
                stat_send[0, g, 0] + near_recv[1, g, 1] + far_recv[1, g],
            ],
            axis=1,
        )
        inverse = 1.0 / total[0:LINES]
        delta = total[LINES:] * inverse
        for i in range(hg):
            h = g * hg + i
            q3, do3, kall, _, cols, vcols = operands(h)
            p = e_all[h] * inverse[i : i + 1]
            weight = p.astype(BF16)
            ds = (p * (dp_all[h] - delta[i : i + 1])).astype(BF16)
            dv = plain(weight, do3)
            dk = plain(ds, q3) * scale
            dq = both_first(ds, kall) * scale
            for kind, (grad, where) in enumerate(((dk, cols), (dv, vcols))):
                for part in range(2):
                    cut = slice(part * (texts // 2), (part + 1) * (texts // 2))
                    text_part[g, part, kind, :, i * HD : (i + 1) * HD] = grad[cut]
                dkv_send[1, :, where] = grad[texts : texts + columns].astype(BF16)
                dkv_own[:, :, where] = grad[texts + columns : texts + columns + tokens].reshape(frames, columns, HD)
                dkv_send[0, :, where] = grad[texts + columns + tokens :].astype(BF16)
            dq_send[1, :, :, cols] = dq[0:tokens].astype(BF16).reshape(frames, columns, HD)
            dq_own[:, :, cols] = dq[tokens : 2 * tokens].reshape(frames, columns, HD)
            dq_send[0, :, :, cols] = dq[2 * tokens :].astype(BF16).reshape(frames, columns, HD)
        core_copy(g).start()
        start_frames(1, g)
        start(dq_copy, row_routes, g)

    def core_copy(g):
        return remote(text_part.at[g, 1 - core], core_recv.at[g], core_s.at[g], core_r.at[g], partner)

    def x_copy(g, source):
        return remote(x_own.at[g], x_recv.at[source], x_s.at[g], x_r.at[source], {"ta": half * nx + g})

    def y_copy(target, source, i):
        return remote(y_own.at[target], y_recv.at[source], y_s.at[i], y_r.at[source], {"ha": spot(core, target, z)})

    def z_copy(target, source, i):
        where = {"ta": (target // RUN) * nx + x, "ha": spot(core, y, lax.rem(target, RUN))}
        return remote(z_own.at[target // RUN], z_recv.at[source], z_s.at[i], z_r.at[source], where)

    def all_copy(c, yy, source, i):
        mine = core * ny + y
        return remote(all_recv.at[mine], all_recv.at[mine], all_s.at[i], all_r.at[source], {"ha": spot(c, yy, z)})

    def text_over_cores(g):
        core_copy(g).wait_recv()
        x_own[g] = text_part[g, core] + core_recv[g]

        @pl.when(g != x)
        def _():
            x_copy(g, x).start()

    def text_over_x(g):
        @pl.when(g == x)
        def _():
            total = x_own[x]
            for source in x_peers:
                x_copy(x, source).wait_recv()
                total = total + x_recv[source]
            part = total.shape[1] // ny
            for target in range(ny):
                y_own[target] = total[:, target * part : (target + 1) * part]
            for i, target in enumerate(y_peers):
                y_copy(target, y, i).start()

    def text_over_y(g):
        @pl.when(g == x)
        def _():
            total = y_own[y]
            for i, source in enumerate(y_peers):
                y_copy(source, source, i).wait_recv()
                total = total + y_recv[source]
            z_own[...] = total
            for i, target in enumerate(z_peers):
                z_copy(target, z_here, i).start()

    def text_over_z(g):
        @pl.when(g == x)
        def _():
            total = z_own[half]
            for i, source in enumerate(z_peers):
                z_copy(source, source, i).wait_recv()
                total = total + z_recv[source]
            all_recv[core * ny + y] = total
            for i, (c, yy) in enumerate(all_peers):
                all_copy(c, yy, core * ny + y, i).start()

    def text_done(g):
        @pl.when(g == x)
        def _():
            for i, (c, yy) in enumerate(all_peers):
                remote(
                    all_recv.at[c * ny + yy],
                    all_recv.at[c * ny + yy],
                    all_s.at[i],
                    all_r.at[c * ny + yy],
                    {"ha": spot(c, yy, z)},
                ).wait_recv()
            text_out[...] = all_recv[...]

    def text_sent():
        for g in range(groups):
            core_copy(g).wait_send()

            @pl.when(g != x)
            def _(g=g):
                x_copy(g, x).wait_send()

        for i, target in enumerate(y_peers):
            y_copy(target, y, i).wait_send()
        for i, target in enumerate(z_peers):
            z_copy(target, z_here, i).wait_send()
        for i, (c, yy) in enumerate(all_peers):
            all_copy(c, yy, core * ny + y, i).wait_send()

    def relay(g):
        @pl.when(g == x)
        def _():
            pass_on(1)

    def fold(g):
        arrived(dkv_copies, frame_routes, g)
        arrived(dq_copy, row_routes, g)
        cols = at(g)
        total = dq_own[:, :, cols] + dq_recv[0, :, :, cols].astype(F32) + dq_recv[1, :, :, cols].astype(F32)
        dq_out[:, 0, :, cols] = total.astype(BF16)
        for base in bases:
            where = at(g, base)
            dkv_out[0, 0, :, where] = (dkv_own[0, :, where] + dkv_recv[0, :, where].astype(F32)).astype(BF16)
            dkv_out[1 : frames - 1, 0, :, where] = dkv_own[1 : frames - 1, :, where].astype(BF16)
            dkv_out[frames - 1, 0, :, where] = (
                dkv_own[frames - 1, :, where] + dkv_recv[1, :, where].astype(F32)
            ).astype(BF16)

    stages = (
        (0, scores),
        (-AHEAD, forward),
        (LAG_GRADS, grads),
        (LAG_RELAY, relay),
        (LAG_TEXT, text_over_cores),
        (LAG_TEXT + 1, text_over_x),
        (LAG_TEXT + 2, text_over_y),
        (LAG_FOLD, fold),
        (LAG_TEXT + 3, text_over_z),
        (LAG_TEXT + 4, text_done),
    )

    def step(s, carry):
        for lag, stage in stages:

            @pl.when((s >= max(lag, 0)) & (s < groups + lag))
            def _(lag=lag, stage=stage):
                stage(s - lag)

        return carry

    lax.fori_loop(0, groups + LAG_TEXT + 4, step, 0)

    def drain(g, carry):
        for make, routes in (
            (frame_copies, frame_routes),
            (row_copies, row_routes),
            (near_copy, row_routes),
            (far_copy, far_routes),
            (dkv_copies, frame_routes),
            (dq_copy, row_routes),
        ):
            sent(make, routes, g)
        return carry

    lax.fori_loop(0, groups, drain, 0)
    passed_on(0)
    passed_on(1)
    text_sent()


def attention_grads(nt, nh, query, key_value, out_grad, text_kv, lanes):
    frames, _, columns, width = query.shape
    tokens = frames * columns
    texts = text_kv.shape[0]
    heads = width // HD
    groups = GROUPS
    gw = width // groups
    nx, ny = nt // 2, nh // (2 * RUN)
    keys = texts + (frames + 2) * columns
    dma = pltpu.SemaphoreType.DMA
    here = pl.BlockSpec(memory_space=pltpu.VMEM)
    away = pl.BlockSpec(memory_space=pl.ANY)
    return pl.pallas_call(
        functools.partial(attention_kernel, nt, nh),
        out_shape=(
            jax.ShapeDtypeStruct(query.shape, BF16),
            jax.ShapeDtypeStruct(key_value.shape, BF16),
            jax.ShapeDtypeStruct((2 * ny, texts // (2 * ny), gw), F32),
        ),
        in_specs=[away, away, away, here, here],
        out_specs=(here, here, here),
        scratch_shapes=[
            pltpu.VMEM((3, frames, columns, width), BF16),
            pltpu.VMEM((3, frames, columns, width), BF16),
            pltpu.VMEM((frames + 2, columns, 2 * width), BF16),
            pltpu.VMEM((keys, 3 * tokens), F32),
            pltpu.VMEM((heads, keys, 3 * tokens), F32),
            pltpu.VMEM((heads, keys, 3 * tokens), F32),
            pltpu.VMEM((2, groups, 2, 2 * LINES, tokens), F32),
            pltpu.VMEM((2, groups, 2, 2 * LINES, tokens), F32),
            pltpu.VMEM((2, groups, 2 * LINES, tokens), F32),
            pltpu.VMEM((2, frames, columns, width), BF16),
            pltpu.VMEM((2, frames, columns, width), BF16),
            pltpu.VMEM((frames, columns, width), F32),
            pltpu.VMEM((2, columns, 2 * width), BF16),
            pltpu.VMEM((2, columns, 2 * width), BF16),
            pltpu.VMEM((frames, columns, 2 * width), F32),
            pltpu.VMEM((2, columns, gw), BF16),
            pltpu.VMEM((2, columns, gw), BF16),
            pltpu.VMEM((groups, 2, 2, texts // 2, gw), F32),
            pltpu.VMEM((groups, 2, texts // 2, gw), F32),
            pltpu.VMEM((groups, 2, texts // 2, gw), F32),
            pltpu.VMEM((nx, 2, texts // 2, gw), F32),
            pltpu.VMEM((ny, 2, texts // (2 * ny), gw), F32),
            pltpu.VMEM((ny, 2, texts // (2 * ny), gw), F32),
            pltpu.VMEM((2, texts // (2 * ny), gw), F32),
            pltpu.VMEM((2 * RUN, texts // (2 * ny), gw), F32),
            pltpu.VMEM((2 * ny, texts // (2 * ny), gw), F32),
            dma((3,)),
            dma((2, 2, groups)),
            dma((2, 2, groups)),
            dma((2, 2, groups)),
            dma((2, 2, groups)),
            dma((2, groups)),
            dma((2, groups)),
            dma((2, groups)),
            dma((2, groups)),
            dma((2, groups)),
            dma((2, groups)),
            dma((2, 2, groups)),
            dma((2, 2, groups)),
            dma((2, 2)),
            dma((2, 2)),
            dma((groups,)),
            dma((groups,)),
            dma((groups,)),
            dma((nx,)),
            dma((ny,)),
            dma((ny,)),
            dma((2 * RUN,)),
            dma((2 * RUN,)),
            dma((2 * ny,)),
            dma((2 * ny,)),
        ],
        compiler_params=pltpu.CompilerParams(collective_id=0, has_side_effects=True, vmem_limit_bytes=60 << 20),
        name="attention_grads",
    )(query, key_value, out_grad, text_kv, lanes)


def lane_limits(tile_reach, text_len, frames, columns):
    time_index, row_index = lax.axis_index("ta"), lax.axis_index("ha")
    first = time_index * frames
    padded = jnp.pad(tile_reach, ((0, 0), (1, 1), (0, 0)), constant_values=-1)
    near = lax.dynamic_slice(padded, (first, row_index, 0), (frames, 3, 2))
    away = jnp.abs(jnp.arange(3, dtype=jnp.int32) - 1)[None, :]
    reach = jnp.where(near[..., 1] >= away, near[..., 0], -1)
    reach = jnp.repeat(reach.T.reshape(-1), columns)
    length = lax.dynamic_slice(text_len, (first, row_index), (frames, 1))[:, 0]
    length = jnp.repeat(jnp.pad(length, (frames, frames)), columns)
    return jnp.stack([reach, length])


def on_device(nt, nh, query, key_value, out_grad, text_kv, tile_reach, text_len):
    lanes = lane_limits(tile_reach, text_len, query.shape[0], query.shape[2])
    query_grad, key_value_grad, text_partial = attention_grads(nt, nh, query, key_value, out_grad, text_kv, lanes)
    share = text_kv.shape[1] // (nt * nh)
    lines = text_partial.reshape(text_kv.shape[0], -1)
    text_grad = lax.dynamic_slice_in_dim(lines, lax.axis_index("ha") * share, share, axis=1).astype(BF16)
    return query_grad, key_value_grad, text_grad


def solution(mesh):
    placed = (
        P("ta", "ha", None, None),
        P("ta", "ha", None, None),
        P("ta", "ha", None, None),
        P(),
        P(),
        P(),
    )
    return jax.shard_map(
        functools.partial(on_device, mesh.shape["ta"], mesh.shape["ha"]),
        mesh=mesh,
        in_specs=placed,
        out_specs=(P("ta", "ha", None, None), P("ta", "ha", None, None), P(None, ("ta", "ha"))),
        check_vma=False,
    )
```

time: 216 us -> 109 us (0.50)
  blocking collectives: 106 us -> 0 us
    unnamed x1 -> x0, blocking collectives: 106 us -> none
where the time goes in v2:
time: 109 us
  Pallas kernels  100 us (92%)
  local copies, waits for them, and re-layouts  7.26 us (7%)
    pallas_call x1, Pallas kernels, attention_grads(): pl.pallas_call(functools.partial(attention_kernel, nt, nh), out_shape=(ja...  100 us
    unnamed x7, local copies, waits for them, and re-layouts  4.46 us

profile of v2, /device:TPU:7, one launch (start us, length us, event | category | flops | bytes accessed | tf_op | source)
XLA Modules:
  0.0 108.9 jit_solution(17480380168516688243)
XLA Ops:
  0.6 0.0 copy-start
  0.7 0.7 copy-done
  1.4 0.2 dynamic-slice_reduce_fusion
  1.6 0.1 pad.9
  1.7 0.9 pad_dynamic-slice_fusion
  2.5 0.1 copy.12
  2.6 0.1 copy.13
  2.7 0.1 fusion
  2.8 0.1 reshape.17
  2.9 0.1 broadcast_in_dim.12
  2.9 0.1 stack_reshape.6
  3.0 0.1 broadcast_in_dim.13
  3.1 0.1 stack_reshape.7
  3.2 0.6 pad_add_fusion.lanes
  3.8 100.3 %attention_grads.1 = (bf16[8,1,16,2560]{3,2,1,0:T(8,128)(2,1)}, bf16[8,1,16,5120]{3,2,1,0:T(8,128)(2,1)}, f32[8,4,640]{2,1,0:T(4,128)}) custom-call(bf16[8,1,16,2560]{3,2,1,0:T(8,128)(2,1)} %q_hbm.1, bf16[8,1,16,5120]{3,2,1,0:T(8,128)(2,1)} %kv_hbm.1, bf16[8,1,16,2560]{3,2,1,0:T(8,128)(2,1)} %do_hbm.1, bf16[32,5120]{1,0:T(8,128)(2,1)} %text.1, ...), custom_call_target="tpu_custom_call" | custom-call | tf_op jit(solution)/shard_map/attention_grads/pallas_call | solution.py:581
  104.1 0.0 copy-start.1
  104.1 1.0 reshape.18
  105.1 0.1 constant_dynamic-slice_fusion
  105.2 0.7 copy.15
  105.9 2.0 %copy.18 = bf16[8,1,16,2560]{3,2,1,0:T(8,128)(2,1)} copy(bf16[8,1,16,2560]{3,2,1,0:T(8,128)(2,1)} %get-tuple-element.14) | data formatting | bytes 1310720
  107.8 0.0 copy-done.1
  107.8 1.1 copy.19
  (1 shorter events, 0.0 us)
Async XLA Ops:
  0.6 0.8 copy-start
  104.1 3.8 %copy-start.1 = (bf16[8,1,16,5120]{3,2,1,0:T(8,128)(2,1)S(1)}, bf16[8,1,16,5120]{3,2,1,0:T(8,128)(2,1)}, u32[]{:S(2)}) copy-start(bf16[8,1,16,5120]{3,2,1,0:T(8,128)(2,1)} %get-tuple-element.15) | copy-start | bytes 3932164

commit v3 on v2

v3 whole, which is shorter than its diff:
```python
import functools
import math

import jax
import jax.numpy as jnp
from jax import lax
from jax.experimental import pallas as pl
from jax.experimental.pallas import tpu as pltpu
from jax.sharding import PartitionSpec as P

HD = 128
MESH = pl.DeviceIdType.MESH
F32 = jnp.float32
BF16 = jnp.bfloat16

CHUNKS = (5, 5, 5, 5)
AHEAD = 2
FIRST = 1
LIMIT = 60
LAG_FOLD = 4
BLOCKS = 4
RUN = 8
LINES = 8


def both_last(a, b):
    return lax.dot_general(a, b, (((1,), (1,)), ((), ())), preferred_element_type=F32)


def both_first(a, b):
    return lax.dot_general(a, b, (((0,), (0,)), ((), ())), preferred_element_type=F32)


def plain(a, b):
    return lax.dot_general(a, b, (((1,), (0,)), ((), ())), preferred_element_type=F32)


def attention_kernel(
    nt,
    nh,
    q_hbm,
    kv_hbm,
    do_hbm,
    text,
    reach,
    length,
    dq_out,
    dkv_out,
    text_out,
    q_all,
    do_all,
    kv_all,
    bias,
    e_all,
    dp_all,
    ds_all,
    stat_send,
    near_recv,
    far_recv,
    dq_send,
    dq_recv,
    dq_own,
    dkv_send,
    dkv_recv,
    dkv_own,
    relay_kv,
    relay_dkv,
    text_part,
    core_recv,
    xy_own,
    xy_recv,
    z_own,
    z_recv,
    all_own,
    all_recv,
    own_sem,
    row_s,
    row_r,
    fr_s,
    fr_r,
    near_s,
    near_r,
    far_s,
    far_r,
    dq_s,
    dq_r,
    dkv_s,
    dkv_r,
    relay_s,
    relay_r,
    core_s,
    core_r,
    xy_s,
    xy_r,
    z_s,
    z_r,
    all_s,
    all_r,
):
    frames, columns = q_all.shape[1], q_all.shape[2]
    width = q_all.shape[3]
    tokens = frames * columns
    texts = text.shape[0]
    heads = width // HD
    starts = [sum(CHUNKS[:c]) for c in range(len(CHUNKS) + 1)]
    hb = heads // BLOCKS
    bw = hb * HD
    scale = 1.0 / math.sqrt(HD)
    keys = texts + (frames + 2) * columns
    ta, ha = lax.axis_index("ta"), lax.axis_index("ha")
    nx = nt // 2
    ny = nh // (2 * RUN)
    half, x = ta // nx, lax.rem(ta, nx)
    core = lax.rem(ha, 2)
    z = lax.rem(ha // 2, RUN)
    y = ha // (2 * RUN)
    first, last = nx - 1, nx
    has_dn, has_up = ha > 0, ha < nh - 1
    has_dn2, has_up2 = ha > 1, ha < nh - 2
    has_prev, has_next = ta > 0, ta < nt - 1
    dn, up = {"ha": ha - 1}, {"ha": ha + 1}
    dn2, up2 = {"ha": ha - 2}, {"ha": ha + 2}
    prev, nxt = {"ta": ta - 1}, {"ta": ta + 1}
    partner = {"ha": ha + 1 - 2 * core}

    def spot(c, yy, zz):
        return (yy * RUN + zz) * 2 + c

    own_copies = [
        pltpu.make_async_copy(q_hbm.at[:, 0], q_all.at[1], own_sem.at[0]),
        pltpu.make_async_copy(do_hbm.at[:, 0], do_all.at[1], own_sem.at[1]),
        pltpu.make_async_copy(kv_hbm.at[:, 0], kv_all.at[pl.ds(1, frames)], own_sem.at[2]),
    ]
    for copy in own_copies:
        copy.start()

    always = ta >= 0
    x_peers = [lax.rem(x + d, nx) for d in range(1, nx)]
    y_peers = [lax.rem(y + d, ny) for d in range(1, ny)]
    xy_peers = [(x, yy) for yy in y_peers] + [(xx, lax.rem(y + d, ny)) for xx in x_peers for d in range(ny)]
    near_peers = [(core, xx, yy) for xx, yy in xy_peers]
    near_peers += [(1 - core, xx, lax.rem(y + d, ny)) for xx in [x] + x_peers for d in range(ny)]
    z_here = half * RUN + z
    z_peers = [lax.rem(z_here + d, 2 * RUN) for d in range(1, 2 * RUN)]
    greet = [(has_dn, dn), (has_up, up), (has_dn2, dn2), (has_up2, up2)]
    greet += [(always, {"ta": half * nx + xx, "ha": spot(c, yy, z)}) for c, xx, yy in near_peers]
    greet += [(always, {"ta": (p // RUN) * nx + x, "ha": spot(core, y, lax.rem(p, RUN))}) for p in z_peers]
    greet += [(ta == first, {"ta": nx + j}) for j in range(nx)]
    greet += [(ta == last, {"ta": j}) for j in range(nx)]
    greet += [(ta < first, {"ta": last}), (ta > last, {"ta": first})]
    barrier = pltpu.get_barrier_semaphore()
    for has, where in greet:

        @pl.when(has)
        def _(where=where):
            pl.semaphore_signal(barrier, inc=1, device_id=where, device_id_type=MESH)

    place = ta * frames
    near_reach = reach[pl.ds(place, frames)].astype(F32)
    near_length = length[pl.ds(pl.multiple_of(place, frames), frames), :].astype(F32)
    token_frame = lax.broadcasted_iota(jnp.int32, (1, tokens), 1) // columns
    row_of = lax.broadcasted_iota(jnp.int32, near_reach.shape, 2)
    pieces = []
    for j, has in ((0, has_dn), (1, always), (2, has_up)):
        found = jnp.sum(jnp.where(row_of == ha + j - 1, near_reach, 0.0), axis=2)
        piece = jnp.full((1, tokens), -1.0, F32)
        for f in range(frames):
            shown = (found[f : f + 1, 1:2] >= abs(j - 1)) & has
            piece = jnp.where((token_frame == f) & shown, found[f : f + 1, 0:1], piece)
        pieces.append(piece)
    limit = jnp.concatenate(pieces, axis=1)
    found = jnp.sum(
        jnp.where(lax.broadcasted_iota(jnp.int32, near_length.shape, 1) == ha, near_length, 0.0), axis=1, keepdims=True
    )
    shown = jnp.zeros((1, tokens), F32)
    for f in range(frames):
        shown = jnp.where(token_frame == f, found[f : f + 1], shown)
    text_limit = jnp.concatenate([jnp.zeros((1, tokens), F32), shown, jnp.zeros((1, tokens), F32)], axis=1)
    line = lax.broadcasted_iota(jnp.int32, (keys, 3 * tokens), 0)
    lane = lax.broadcasted_iota(jnp.int32, (keys, 3 * tokens), 1)
    query_frame = lax.rem(lane, tokens) // columns
    key_frame = (line - texts + columns) // columns - 2
    gap = jnp.abs(key_frame - query_frame).astype(F32)
    inside = ((key_frame >= 0) | has_prev) & ((key_frame < frames) | has_next)
    latent_seen = (line >= texts) & inside & (gap <= limit)
    text_seen = (line < texts) & (line.astype(F32) < text_limit)
    bias[...] = jnp.where(latent_seen | text_seen, 0.0, -1e30)

    pl.semaphore_wait(barrier, sum(has.astype(jnp.int32) for has, _ in greet))

    def at(c):
        return pl.ds(starts[c] * HD, CHUNKS[c] * HD)

    def of(b, base=0):
        return pl.ds(pl.multiple_of(base + b * bw, HD), bw)

    def remote(src, dst, send, recv, where):
        return pltpu.make_async_remote_copy(
            src_ref=src,
            dst_ref=dst,
            send_sem=send,
            recv_sem=recv,
            device_id=where,
            device_id_type=MESH,
        )

    def row_copies(g, side, where):
        slot = 0 if side == 0 else 2
        return [
            remote(
                hbm.at[:, 0, :, at(g)], ref.at[slot, :, :, at(g)], row_s.at[side, i, g], row_r.at[side, i, g], where
            )
            for i, (hbm, ref) in enumerate(((q_hbm, q_all), (do_hbm, do_all)))
        ]

    bases = (0, width)

    def kv_source(g, side, base):
        return kv_hbm.at[frames - 1 if side == 0 else 0, 0, :, of(g, base)]

    def kv_target(g, side, base):
        return kv_all.at[0 if side == 0 else frames + 1, :, of(g, base)]

    def dkv_source(g, side, base):
        return dkv_send.at[side, :, of(g, base)]

    def dkv_target(g, side, base):
        return dkv_recv.at[side, :, of(g, base)]

    def frame_copies(g, side, where):
        return [
            remote(
                kv_source(g, side, base), kv_target(g, side, base), fr_s.at[side, i, g], fr_r.at[side, i, g], where
            )
            for i, base in enumerate(bases)
        ]

    def dkv_copies(g, side, where):
        return [
            remote(
                dkv_source(g, side, base), dkv_target(g, side, base), dkv_s.at[side, i, g], dkv_r.at[side, i, g], where
            )
            for i, base in enumerate(bases)
        ]

    def to_relay(kind, g, side, where):
        source, send, held = ((kv_source, fr_s, relay_kv), (dkv_source, dkv_s, relay_dkv))[kind]
        return [
            remote(source(g, side, base), held.at[i], send.at[side, i, g], relay_r.at[kind, i], where)
            for i, base in enumerate(bases)
        ]

    def from_relay(kind, g, side, where):
        held, target, recv = ((relay_kv, kv_target, fr_r), (relay_dkv, dkv_target, dkv_r))[kind]
        return [
            remote(held.at[i], target(g, side, base), relay_s.at[kind, i], recv.at[side, i, g], where)
            for i, base in enumerate(bases)
        ]

    def near_copy(g, side, where):
        return [remote(stat_send.at[side, g], near_recv.at[side, g], near_s.at[side, g], near_r.at[side, g], where)]

    def far_copy(g, side, where):
        return [remote(stat_send.at[side, g, 0], far_recv.at[side, g], far_s.at[side, g], far_r.at[side, g], where)]

    def dq_copy(g, side, where):
        return [
            remote(
                dq_send.at[side, :, :, at(g)], dq_recv.at[side, :, :, at(g)], dq_s.at[side, g], dq_r.at[side, g], where
            )
        ]

    row_routes = ((0, has_up, up, has_dn), (1, has_dn, dn, has_up))
    far_routes = ((0, has_up2, up2, has_dn2), (1, has_dn2, dn2, has_up2))
    frame_routes = ((0, has_next, nxt, has_prev), (1, has_prev, prev, has_next))
    crossings = ((0, ta == first, nxt), (1, ta == last, prev))

    def start(make, routes, g):
        for side, has, where, _ in routes:

            @pl.when(has)
            def _(side=side, where=where):
                for copy in make(g, side, where):
                    copy.start()

    def arrived(make, routes, g):
        for side, _, where, has in routes:

            @pl.when(has)
            def _(side=side, where=where):
                for copy in make(g, side, where):
                    copy.wait_recv()

    def sent(make, routes, g):
        for side, has, where, _ in routes:

            @pl.when(has)
            def _(side=side, where=where):
                for copy in make(g, side, where):
                    copy.wait_send()

    def start_frames(kind, g):
        make = (frame_copies, dkv_copies)[kind]
        for (side, has, where, _), (_, crosses, _) in zip(frame_routes, crossings):
            relayed = crosses & (g != x)

            @pl.when(has & jnp.logical_not(relayed))
            def _(side=side, where=where):
                for copy in make(g, side, where):
                    copy.start()

            @pl.when(relayed)
            def _(side=side):
                for copy in to_relay(kind, g, side, {"ta": half * nx + g}):
                    copy.start()

    relays = ((0, (half == 0) & (ta != first), {"ta": last}), (1, (half == 1) & (ta != last), {"ta": first}))

    def pass_on(kind):
        for side, has, where in relays:

            @pl.when(has)
            def _(side=side, where=where):
                for copy in to_relay(kind, x, side, where):
                    copy.wait_recv()
                for copy in from_relay(kind, x, side, where):
                    copy.start()

    def passed_on(kind):
        for side, has, where in relays:

            @pl.when(has)
            def _(side=side, where=where):
                for copy in from_relay(kind, x, side, where):
                    copy.wait_send()

    def forward(g):
        start(row_copies, row_routes, g)

    for b in range(BLOCKS):
        start_frames(0, b)
    for g in range(FIRST):
        forward(g)

    for side, _, _, has in row_routes:

        @pl.when(jnp.logical_not(has))
        def _(side=side):
            slot = 0 if side == 0 else 2
            q_all[slot] = jnp.zeros(q_all.shape[1:], BF16)
            do_all[slot] = jnp.zeros(do_all.shape[1:], BF16)
            near_recv[side, :, 0] = jnp.zeros((len(CHUNKS),) + near_recv.shape[3:], F32)
            near_recv[side, :, 1] = jnp.ones((len(CHUNKS),) + near_recv.shape[3:], F32)
            dq_recv[side] = jnp.zeros(dq_recv.shape[1:], BF16)

    for side, _, _, has in far_routes:

        @pl.when(jnp.logical_not(has))
        def _(side=side):
            far_recv[side] = jnp.zeros(far_recv.shape[1:], F32)

    for side, _, _, has in frame_routes:

        @pl.when(jnp.logical_not(has))
        def _(side=side):
            slot = 0 if side == 0 else frames + 1
            kv_all[slot] = jnp.zeros(kv_all.shape[1:], BF16)
            dkv_recv[side] = jnp.zeros(dkv_recv.shape[1:], BF16)

    pass_on(0)
    for g in range(FIRST, AHEAD):
        forward(g)
    for copy in own_copies:
        copy.wait()

    def operands(h):
        cols, vcols = pl.ds(h * HD, HD), pl.ds(width + h * HD, HD)
        q3 = q_all[:, :, :, cols].reshape(3 * tokens, HD)
        do3 = do_all[:, :, :, cols].reshape(3 * tokens, HD)
        kall = jnp.concatenate([text[:, cols], kv_all[:, :, cols].reshape(-1, HD)], axis=0)
        vall = jnp.concatenate([text[:, vcols], kv_all[:, :, vcols].reshape(-1, HD)], axis=0)
        return q3, do3, kall, vall, cols, vcols

    def finished(g):
        return [b for b in range(BLOCKS) if starts[g] < (b + 1) * hb <= starts[g + 1]]

    def scores(g):
        for b in range(BLOCKS):
            if starts[g] <= b * hb < starts[g + 1]:
                arrived(frame_copies, frame_routes, b)
        arrived(row_copies, row_routes, g)
        sums = []
        hg = CHUNKS[g]
        for h in range(starts[g], starts[g + 1]):
            q3, do3, kall, vall, _, _ = operands(h)
            s = both_last(kall, q3)
            dp = both_last(vall, do3)
            e = jnp.exp(s * scale + bias[...])
            e_all[h] = e
            dp_all[h] = dp
            sums.append((jnp.sum(e, axis=0, keepdims=True), jnp.sum(e * dp, axis=0, keepdims=True)))
        filler = [jnp.ones((1, tokens), F32)] * (LINES - hg)
        blocks = []
        for part in range(3):
            cut = slice(part * tokens, (part + 1) * tokens)
            lines = [a[:, cut] for a, _ in sums] + filler + [b[:, cut] for _, b in sums] + filler
            blocks.append(jnp.concatenate(lines, axis=0))
        stat_send[0, g, 0] = blocks[2]
        stat_send[1, g, 0] = blocks[0]
        stat_send[0, g, 1] = blocks[1]
        stat_send[1, g, 1] = blocks[1]
        start(near_copy, row_routes, g)
        start(far_copy, far_routes, g)

    def grads(g):
        arrived(near_copy, row_routes, g)
        arrived(far_copy, far_routes, g)
        total = jnp.concatenate(
            [
                stat_send[1, g, 0] + near_recv[0, g, 1] + far_recv[0, g],
                stat_send[0, g, 1] + near_recv[0, g, 0] + near_recv[1, g, 0],
                stat_send[0, g, 0] + near_recv[1, g, 1] + far_recv[1, g],
            ],
            axis=1,
        )
        inverse = 1.0 / total[0:LINES]
        delta = total[LINES:] * inverse
        for i, h in enumerate(range(starts[g], starts[g + 1])):
            q3, do3, kall, _, cols, vcols = operands(h)
            p = e_all[h] * inverse[i : i + 1]
            weight = p.astype(BF16)
            ds = (p * (dp_all[h] - delta[i : i + 1])).astype(BF16)
            ds_all[i] = ds
            dv = plain(weight, do3)
            dk = plain(ds, q3) * scale
            b, lanes = h // hb, slice(h % hb * HD, (h % hb + 1) * HD)
            for kind, (grad, where) in enumerate(((dk, cols), (dv, vcols))):
                for part in range(2):
                    cut = slice(part * (texts // 2), (part + 1) * (texts // 2))
                    text_part[b, part, kind, :, lanes] = grad[cut]
                dkv_send[1, :, where] = grad[texts : texts + columns].astype(BF16)
                dkv_own[:, :, where] = grad[texts + columns : texts + columns + tokens].reshape(frames, columns, HD)
                dkv_send[0, :, where] = grad[texts + columns + tokens :].astype(BF16)
        for b in finished(g):
            core_copy(b).start()
            start_frames(1, b)
        for i, h in enumerate(range(starts[g], starts[g + 1])):
            _, _, kall, _, cols, _ = operands(h)
            dq = both_first(ds_all[i], kall) * scale
            dq_send[1, :, :, cols] = dq[0:tokens].astype(BF16).reshape(frames, columns, HD)
            dq_own[:, :, cols] = dq[tokens : 2 * tokens].reshape(frames, columns, HD)
            dq_send[0, :, :, cols] = dq[2 * tokens :].astype(BF16).reshape(frames, columns, HD)
        start(dq_copy, row_routes, g)

    def core_copy(g):
        return remote(text_part.at[g, 1 - core], core_recv.at[g], core_s.at[g], core_r.at[g], partner)

    def line_of(xx, yy):
        return xx * ny + yy

    def xy_copy(b, xx, yy, source, i):
        where = {"ta": half * nx + xx, "ha": spot(core, yy, z)}
        return remote(xy_own.at[b, line_of(xx, yy)], xy_recv.at[b, source], xy_s.at[b, i], xy_r.at[b, source], where)

    def z_copy(b, target, source, i):
        where = {"ta": (target // RUN) * nx + x, "ha": spot(core, y, lax.rem(target, RUN))}
        return remote(z_own.at[b, target // RUN], z_recv.at[b, source], z_s.at[b, i], z_r.at[b, source], where)

    def all_copy(b, c, yy, source, i):
        where = {"ta": half * nx + b, "ha": spot(c, yy, z)}
        return remote(all_own.at[b], all_recv.at[source], all_s.at[b, i], all_r.at[source], where)

    other_places = [(core, yy) for yy in y_peers] + [(1 - core, lax.rem(y + d, ny)) for d in range(ny)]
    my_line = core * nx * ny + line_of(x, y)

    def text_over_cores(b):
        core_copy(b).wait_recv()
        total = text_part[b, core] + core_recv[b]
        for k in range(nx * ny):
            xy_own[b, k] = total[:, k : k + 1]
        for i, (xx, yy) in enumerate(xy_peers):
            xy_copy(b, xx, yy, line_of(x, y), i).start()

    def text_over_xy(b):
        total = xy_own[b, line_of(x, y)]
        for xx, yy in xy_peers:
            xy_copy(b, x, y, line_of(xx, yy), 0).wait_recv()
        for xx, yy in xy_peers:
            total = total + xy_recv[b, line_of(xx, yy)]
        z_own[b] = total
        for i, target in enumerate(z_peers):
            z_copy(b, target, z_here, i).start()

    def text_over_z(b):
        total = z_own[b, half]
        for source in z_peers:
            z_copy(b, z_here, source, 0).wait_recv()
        for source in z_peers:
            total = total + z_recv[b, source]
        all_own[b] = total
        for i, (c, yy) in enumerate(other_places):
            all_copy(b, c, yy, my_line, i).start()

        @pl.when(b != x)
        def _():
            all_copy(b, core, y, my_line, 2 * ny - 1).start()

        @pl.when(b == x)
        def _():
            all_recv[my_line] = total

    def text_done(b):
        @pl.when(b == x)
        def _():
            for c, xx, yy in near_peers:
                all_copy(b, core, y, c * nx * ny + line_of(xx, yy), 0).wait_recv()
            share = text_out.shape[0]
            spread = all_recv.shape[2]
            where = lax.broadcasted_iota(jnp.int32, (16, spread), 1) - ha * share
            pick = jnp.where(where == lax.broadcasted_iota(jnp.int32, (16, spread), 0), 1.0, 0.0)
            mine = lax.dot_general(
                pick,
                all_recv[...].reshape(-1, spread),
                (((1,), (1,)), ((), ())),
                precision=lax.Precision.HIGHEST,
                preferred_element_type=F32,
            )
            text_out[...] = mine[0:share].astype(BF16)

    def text_sent():
        for b in range(BLOCKS):
            core_copy(b).wait_send()
            for i, (xx, yy) in enumerate(xy_peers):
                xy_copy(b, xx, yy, line_of(x, y), i).wait_send()
            for i, target in enumerate(z_peers):
                z_copy(b, target, z_here, i).wait_send()
            for i, (c, yy) in enumerate(other_places):
                all_copy(b, c, yy, my_line, i).wait_send()

            @pl.when(b != x)
            def _(b=b):
                all_copy(b, core, y, my_line, 2 * ny - 1).wait_send()

    def relay(g):
        @pl.when(g == x)
        def _():
            pass_on(1)

    def fold_rows(c):
        arrived(dq_copy, row_routes, c)
        cols = at(c)
        total = dq_own[:, :, cols] + dq_recv[0, :, :, cols].astype(F32) + dq_recv[1, :, :, cols].astype(F32)
        dq_out[:, 0, :, cols] = total.astype(BF16)

    def fold_frames(b):
        arrived(dkv_copies, frame_routes, b)
        for base in bases:
            where = of(b, base)
            dkv_out[0, 0, :, where] = (dkv_own[0, :, where] + dkv_recv[0, :, where].astype(F32)).astype(BF16)
            dkv_out[1 : frames - 1, 0, :, where] = dkv_own[1 : frames - 1, :, where].astype(BF16)
            dkv_out[frames - 1, 0, :, where] = (
                dkv_own[frames - 1, :, where] + dkv_recv[1, :, where].astype(F32)
            ).astype(BF16)

    count = len(CHUNKS)
    ready = [next(c for c in range(count) if b in finished(c)) + 1 for b in range(BLOCKS)]
    for s in range(count + 6):
        if s < count:
            scores(s)
        if AHEAD <= s + AHEAD < count:
            forward(s + AHEAD)
        if 0 <= s - 1 < count:
            grads(s - 1)
        for lag, stage in (
            (1, text_over_cores),
            (1, relay),
            (2, text_over_xy),
            (3, text_over_z),
            (LAG_FOLD - 1, fold_frames),
            (LAG_FOLD, fold_rows),
            (4, text_done),
        ):
            for b in range(count if stage is fold_rows else BLOCKS):
                if s == lag + (b if stage is fold_rows else ready[b]):
                    stage(b)

    for c in range(count):
        for make, routes in ((row_copies, row_routes), (near_copy, row_routes), (far_copy, far_routes), (dq_copy, row_routes)):
            sent(make, routes, c)
    for b in range(BLOCKS):
        for make in (frame_copies, dkv_copies):
            sent(make, frame_routes, b)
    passed_on(0)
    passed_on(1)
    text_sent()


def attention_grads(nt, nh, query, key_value, out_grad, text_kv, reach, length):
    frames, _, columns, width = query.shape
    tokens = frames * columns
    texts = text_kv.shape[0]
    heads = width // HD
    count = len(CHUNKS)
    bw = width // BLOCKS
    nx, ny = nt // 2, nh // (2 * RUN)
    keys = texts + (frames + 2) * columns
    dma = pltpu.SemaphoreType.DMA
    here = pl.BlockSpec(memory_space=pltpu.VMEM)
    away = pl.BlockSpec(memory_space=pl.ANY)
    return pl.pallas_call(
        functools.partial(attention_kernel, nt, nh),
        out_shape=(
            jax.ShapeDtypeStruct(query.shape, BF16),
            jax.ShapeDtypeStruct(key_value.shape, BF16),
            jax.ShapeDtypeStruct((2 * width // (nt * nh), texts), BF16),
        ),
        in_specs=[away, away, away, here, here, here],
        out_specs=(here, here, here),
        scratch_shapes=[
            pltpu.VMEM((3, frames, columns, width), BF16),
            pltpu.VMEM((3, frames, columns, width), BF16),
            pltpu.VMEM((frames + 2, columns, 2 * width), BF16),
            pltpu.VMEM((keys, 3 * tokens), F32),
            pltpu.VMEM((heads, keys, 3 * tokens), F32),
            pltpu.VMEM((heads, keys, 3 * tokens), F32),
            pltpu.VMEM((max(CHUNKS), keys, 3 * tokens), BF16),
            pltpu.VMEM((2, count, 2, 2 * LINES, tokens), F32),
            pltpu.VMEM((2, count, 2, 2 * LINES, tokens), F32),
            pltpu.VMEM((2, count, 2 * LINES, tokens), F32),
            pltpu.VMEM((2, frames, columns, width), BF16),
            pltpu.VMEM((2, frames, columns, width), BF16),
            pltpu.VMEM((frames, columns, width), F32),
            pltpu.VMEM((2, columns, 2 * width), BF16),
            pltpu.VMEM((2, columns, 2 * width), BF16),
            pltpu.VMEM((frames, columns, 2 * width), F32),
            pltpu.VMEM((2, columns, bw), BF16),
            pltpu.VMEM((2, columns, bw), BF16),
            pltpu.VMEM((BLOCKS, 2, 2, texts // 2, bw), F32),
            pltpu.VMEM((BLOCKS, 2, texts // 2, bw), F32),
            pltpu.VMEM((BLOCKS, nx * ny, 2, 1, bw), F32),
            pltpu.VMEM((BLOCKS, nx * ny, 2, 1, bw), F32),
            pltpu.VMEM((BLOCKS, 2, 1, bw), F32),
            pltpu.VMEM((BLOCKS, 2 * RUN, 1, bw), F32),
            pltpu.VMEM((BLOCKS, 1, bw), F32),
            pltpu.VMEM((texts, 1, bw), F32),
            dma((3,)),
            dma((2, 2, count)),
            dma((2, 2, count)),
            dma((2, 2, BLOCKS)),
            dma((2, 2, BLOCKS)),
            dma((2, count)),
            dma((2, count)),
            dma((2, count)),
            dma((2, count)),
            dma((2, count)),
            dma((2, count)),
            dma((2, 2, BLOCKS)),
            dma((2, 2, BLOCKS)),
            dma((2, 2)),
            dma((2, 2)),
            dma((BLOCKS,)),
            dma((BLOCKS,)),
            dma((BLOCKS, nx * ny)),
            dma((BLOCKS, nx * ny)),
            dma((BLOCKS, 2 * RUN)),
            dma((BLOCKS, 2 * RUN)),
            dma((BLOCKS, 2 * ny)),
            dma((texts,)),
        ],
        compiler_params=pltpu.CompilerParams(collective_id=0, has_side_effects=True, vmem_limit_bytes=LIMIT << 20),
        name="attention_grads",
    )(query, key_value, out_grad, text_kv, reach, length)


def on_device(nt, nh, query, key_value, out_grad, text_kv, tile_reach, text_len):
    query_grad, key_value_grad, text_grad = attention_grads(
        nt, nh, query, key_value, out_grad, text_kv, jnp.transpose(tile_reach, (0, 2, 1)), text_len
    )
    return query_grad, key_value_grad, text_grad.T


def solution(mesh):
    placed = (
        P("ta", "ha", None, None),
        P("ta", "ha", None, None),
        P("ta", "ha", None, None),
        P(),
        P(),
        P(),
    )
    return jax.shard_map(
        functools.partial(on_device, mesh.shape["ta"], mesh.shape["ha"]),
        mesh=mesh,
        in_specs=placed,
        out_specs=(P("ta", "ha", None, None), P("ta", "ha", None, None), P(None, ("ta", "ha"))),
        check_vma=False,
    )
```

time: 109 us -> 104 us (0.954)
  local copies, waits for them, and re-layouts: 7.26 us -> 3.73 us
    reshape x2 -> x0, local copies, waits for them, and re-layouts: 1.11 us -> none  [the longest x1 1.03 us: on_device(): lines = text_partial.reshape(text_kv.shape[0], -1)]
where the time goes in v3:
time: 104 us
  Pallas kernels  99.8 us (96%)
  local copies, waits for them, and re-layouts  3.73 us (4%)
    pallas_call x1, Pallas kernels, attention_grads(): pl.pallas_call(functools.partial(attention_kernel, nt, nh), out_shape=(ja...  99.8 us
    unnamed x7, local copies, waits for them, and re-layouts  3.73 us

profile of v3, /device:TPU:7, one launch (start us, length us, event | category | flops | bytes accessed | tf_op | source)
XLA Modules:
  0.0 104.2 jit_solution(15078653822542068441)
XLA Ops:
  0.6 99.8 %attention_grads.1 = (bf16[8,1,16,2560]{3,2,1,0:T(8,128)(2,1)}, bf16[8,1,16,5120]{3,2,1,0:T(8,128)(2,1)}, bf16[10,32]{1,0:T(8,128)(2,1)}) custom-call(bf16[8,1,16,2560]{3,2,1,0:T(8,128)(2,1)} %q_hbm.1, bf16[8,1,16,5120]{3,2,1,0:T(8,128)(2,1)} %kv_hbm.1, bf16[8,1,16,2560]{3,2,1,0:T(8,128)(2,1)} %do_hbm.1, bf16[32,5120]{1,0:T(8,128)(2,1)} %text.1, ...), custom_call_target="tpu_custom_call" | custom-call | tf_op jit(solution)/shard_map/attention_grads/pallas_call | solution.py:610
  100.4 0.0 copy-start
  100.4 2.1 %copy.12 = bf16[8,1,16,2560]{3,2,1,0:T(8,128)(2,1)} copy(bf16[8,1,16,2560]{3,2,1,0:T(8,128)(2,1)} %get-tuple-element.12) | data formatting | bytes 1310720
  102.5 0.0 copy-done
  102.5 0.0 copy-start.1
  102.5 1.1 %copy.13 = bf16[8,1,16,5120]{3,2,1,0:T(8,128)(2,1)} copy(bf16[8,1,16,5120]{3,2,1,0:T(8,128)(2,1)S(1)} %copy-done) | data formatting | bytes 2621440
  103.6 0.0 copy-done.1
  103.6 0.6 copy.14
Async XLA Ops:
  100.4 2.1 %copy-start = (bf16[8,1,16,5120]{3,2,1,0:T(8,128)(2,1)S(1)}, bf16[8,1,16,5120]{3,2,1,0:T(8,128)(2,1)}, u32[]{:S(2)}) copy-start(bf16[8,1,16,5120]{3,2,1,0:T(8,128)(2,1)} %get-tuple-element.13) | copy-start | bytes 3932164
  102.5 1.1 %copy-start.1 = (bf16[10,32]{1,0:T(8,128)(2,1)S(1)}, bf16[10,32]{1,0:T(8,128)(2,1)}, u32[]{:S(2)}) copy-start(bf16[10,32]{1,0:T(8,128)(2,1)} %get-tuple-element.8) | copy-start | bytes 1924

commit v4 on v3

--- a/solution.py
+++ b/solution.py
@@ -14,10 +14,10 @@
 BF16 = jnp.bfloat16
 
 CHUNKS = (5, 5, 5, 5)
-AHEAD = 2
+AHEAD = 3
 FIRST = 1
 LIMIT = 60
-LAG_FOLD = 4
+LAG_GRADS = 2
 BLOCKS = 4
 RUN = 8
 LINES = 8
@@ -563,21 +563,21 @@
             ).astype(BF16)
 
     count = len(CHUNKS)
-    ready = [next(c for c in range(count) if b in finished(c)) + 1 for b in range(BLOCKS)]
-    for s in range(count + 6):
+    ready = [next(c for c in range(count) if b in finished(c)) + LAG_GRADS for b in range(BLOCKS)]
+    for s in range(count + LAG_GRADS + 5):
         if s < count:
             scores(s)
         if AHEAD <= s + AHEAD < count:
             forward(s + AHEAD)
-        if 0 <= s - 1 < count:
-            grads(s - 1)
+        if 0 <= s - LAG_GRADS < count:
+            grads(s - LAG_GRADS)
         for lag, stage in (
             (1, text_over_cores),
             (1, relay),
             (2, text_over_xy),
             (3, text_over_z),
-            (LAG_FOLD - 1, fold_frames),
-            (LAG_FOLD, fold_rows),
+            (3, fold_frames),
+            (LAG_GRADS + 3, fold_rows),
             (4, text_done),
         ):
             for b in range(count if stage is fold_rows else BLOCKS):

time: 104 us -> 103 us (level)
  Pallas kernels: 99.8 us -> 98.4 us
    pallas_call x1, Pallas kernels: 99.8 us -> 98.4 us  [attention_grads(): pl.pallas_call(functools.partial(attention_kernel, nt, nh), out_shape=(ja...]
where the time goes in v4:
time: 103 us
  Pallas kernels  98.4 us (96%)
  local copies, waits for them, and re-layouts  3.73 us (4%)
    pallas_call x1, Pallas kernels, attention_grads(): pl.pallas_call(functools.partial(attention_kernel, nt, nh), out_shape=(ja...  98.4 us
    unnamed x7, local copies, waits for them, and re-layouts  3.73 us

profile of v4, /device:TPU:7, one launch (start us, length us, event | category | flops | bytes accessed | tf_op | source)
XLA Modules:
  0.0 102.8 jit_solution(667676228139932700)
XLA Ops:
  0.6 98.4 %attention_grads.1 = (bf16[8,1,16,2560]{3,2,1,0:T(8,128)(2,1)}, bf16[8,1,16,5120]{3,2,1,0:T(8,128)(2,1)}, bf16[10,32]{1,0:T(8,128)(2,1)}) custom-call(bf16[8,1,16,2560]{3,2,1,0:T(8,128)(2,1)} %q_hbm.1, bf16[8,1,16,5120]{3,2,1,0:T(8,128)(2,1)} %kv_hbm.1, bf16[8,1,16,2560]{3,2,1,0:T(8,128)(2,1)} %do_hbm.1, bf16[32,5120]{1,0:T(8,128)(2,1)} %text.1, ...), custom_call_target="tpu_custom_call" | custom-call | tf_op jit(solution)/shard_map/attention_grads/pallas_call | solution.py:610
  99.0 0.0 copy-start
  99.1 2.1 %copy.12 = bf16[8,1,16,2560]{3,2,1,0:T(8,128)(2,1)} copy(bf16[8,1,16,2560]{3,2,1,0:T(8,128)(2,1)} %get-tuple-element.12) | data formatting | bytes 1310720
  101.1 0.0 copy-done
  101.1 0.0 copy-start.1
  101.1 1.1 %copy.13 = bf16[8,1,16,5120]{3,2,1,0:T(8,128)(2,1)} copy(bf16[8,1,16,5120]{3,2,1,0:T(8,128)(2,1)S(1)} %copy-done) | data formatting | bytes 2621440
  102.2 0.0 copy-done.1
  102.2 0.6 copy.14
Async XLA Ops:
  99.0 2.1 %copy-start = (bf16[8,1,16,5120]{3,2,1,0:T(8,128)(2,1)S(1)}, bf16[8,1,16,5120]{3,2,1,0:T(8,128)(2,1)}, u32[]{:S(2)}) copy-start(bf16[8,1,16,5120]{3,2,1,0:T(8,128)(2,1)} %get-tuple-element.13) | copy-start | bytes 3932164
  101.1 1.1 %copy-start.1 = (bf16[10,32]{1,0:T(8,128)(2,1)S(1)}, bf16[10,32]{1,0:T(8,128)(2,1)}, u32[]{:S(2)}) copy-start(bf16[10,32]{1,0:T(8,128)(2,1)} %get-tuple-element.8) | copy-start | bytes 1924
